TPU v7x, 1024 devices: a whole 8x8x8 slice. The times are simulated.
1024 devices in a mesh: pipe: 64 (over z, x_hi, core), dp: 16 (over x_lo, y).
Axes of the slice: x: 8 (x_hi: 4, x_lo: 2; x = x_hi * 2 + x_lo), y: 8, z: 8, core: 2. Of those that a mesh axis runs over, the one named last changes fastest.
Arguments:
- saved: bfloat16 [64, 4096, 1024], P('pipe', 'dp'), may hold values from -6 to 6
- passed: bfloat16 [64, 4096, 1024], P('pipe', 'dp'), may hold values from -6 to 6
- weight: bfloat16 [64, 1024, 1024], P('pipe'), may hold values from -0.1875 to 0.1875
- master: float32 [64, 1024, 1024], P('pipe', 'dp'), may hold values from -0.1875 to 0.1875
- moment_one: float32 [64, 1024, 1024], P('pipe', 'dp'), may hold values from -6 to 6
- moment_two: float32 [64, 1024, 1024], P('pipe', 'dp'), may hold values from 0.5 to 4
- counts: int32 [32], P('dp'), may hold values from 1 to 128, 3072 in all
Outputs:
- input_grad: bfloat16 [64, 4096, 1024], P('pipe', 'dp')
- master_new: float32 [64, 1024, 1024], P('pipe', 'dp')
- moment_one_new: float32 [64, 1024, 1024], P('pipe', 'dp')
- moment_two_new: float32 [64, 1024, 1024], P('pipe', 'dp')
Inputs may be any that keep to these rules, and one draw needn't show every extreme that they name: `counts`: each count is at most 128, and some micro-batch has all 128 slots live.
All inputs are finite; a program needn't handle non-finite values. No bound on the sum of `counts` on one device may be relied on, other than what follows from the above.
Results may differ from a plain program's by a relative error of at most 0.0049.
Values may be sent and summed in bfloat16 or wider, within the bound.
No kernel may reach another device: no remote copies, remote signals or barrier semaphores. Data moves between devices by JAX's collectives and lax.ppermute only.
A program may use at most 32 MiB of HBM per device.

v0:
```python
import math

import jax
import jax.numpy as jnp
from jax import lax
from jax.sharding import PartitionSpec as P

corr_first = 0.9999734386011124
corr_second = 0.09520785288696


def passed_along(x, axis, by):
    size = lax.axis_size(axis)
    return lax.ppermute(x, axis, [(i, (i + by) % size) for i in range(size)])


def local(saved, passed, weight, master, moment_one, moment_two, counts):
    acts = saved[0]
    w_section = weight[0]
    upstream = passed_along(passed, "pipe", -1)[0]
    rows = acts.shape[0]
    block = rows // counts.shape[0]
    live = jnp.arange(rows) % block < jnp.repeat(counts, block)
    pre = jnp.dot(acts, w_section, preferred_element_type=jnp.float32)
    _, back = jax.vjp(jax.nn.gelu, pre)
    local_grad = back(upstream.astype(jnp.float32))[0]
    local_grad = jnp.where(live[:, None], local_grad, jnp.float32(0.0)).astype(jnp.bfloat16)
    in_grad = lax.dot_general(
        local_grad, w_section, (((1,), (1,)), ((), ())), preferred_element_type=jnp.float32
    ).astype(jnp.bfloat16)
    scale = 1.0 / math.sqrt(lax.axis_size("dp") * rows)
    total = lax.dot_general(
        acts, local_grad, (((0,), (0,)), ((), ())), preferred_element_type=jnp.float32
    )
    summed = lax.psum_scatter(
        total.astype(jnp.bfloat16), "dp", scatter_dimension=0, tiled=True
    ).astype(jnp.float32)
    grad = summed * scale
    master_section = master[0]
    first_new = 0.9 * moment_one[0] + 0.1 * grad
    second_new = 0.999 * moment_two[0] + 0.001 * grad * grad
    direction = first_new / corr_first / (jnp.sqrt(second_new / corr_second) + 1e-08)
    master_out = master_section - 0.01 * (direction + 0.1 * master_section)
    return (in_grad[None], master_out[None], first_new[None], second_new[None])


def solution(mesh):
    in_specs = (
        P("pipe", "dp", None),
        P("pipe", "dp", None),
        P("pipe", None, None),
        P("pipe", "dp", None),
        P("pipe", "dp", None),
        P("pipe", "dp", None),
        P("dp"),
    )
    out_specs = (
        P("pipe", "dp", None),
        P("pipe", "dp", None),
        P("pipe", "dp", None),
        P("pipe", "dp", None),
    )
    return jax.shard_map(local, mesh=mesh, in_specs=in_specs, out_specs=out_specs, check_vma=False)
```

profile of v0, /device:TPU:14, one launch (start us, length us, event | category | flops | bytes accessed | tf_op | source)
XLA Modules:
  0.0 142.9 jit_solution(870471583956155835)
XLA Ops:
  7.2 0.0 copy-start
  7.2 0.0 reduce-scatter.4.cloned.1.call-start
  7.2 3.8 %collective-permute-start = (bf16[1,256,1024]{2,1,0:T(8,128)(2,1)}, bf16[1,256,1024]{2,1,0:T(8,128)(2,1)S(1)}, u32[]{:S(2)}, u32[]{:S(2)}) collective-permute-start(bf16[1,256,1024]{2,1,0:T(8,128)(2,1)} %param.8), channel_id=1, source_target_pairs={{0,1008},{16,0},{32,16},{48,32},{64,48},{80,64},{96,80},{112,96},{... | collective-permute-start | bytes 1572872 | tf_op jit(solution)/shard_map/ppermute | solution.py:14
  11.0 0.7 fusion.35
  11.7 0.0 copy-start.1
  11.7 6.3 %collective-permute-done = bf16[1,256,1024]{2,1,0:T(8,128)(2,1)S(1)} collective-permute-done((bf16[1,256,1024]{2,1,0:T(8,128)(2,1)}, bf16[1,256,1024]{2,1,0:T(8,128)(2,1)S(1)}, u32[]{:S(2)}, u32[]{:S(2)}) %collective-permute-start) | collective-permute-done | bytes 524320 | tf_op jit(solution)/shard_map/ppermute | solution.py:14
  18.1 0.0 copy-done
  18.1 2.5 %fusion.13 = bf16[256,1024]{1,0:T(8,128)(2,1)S(1)} fusion(bf16[1,256,1024]{2,1,0:T(8,128)(2,1)S(1)} %collective-permute-done, bf16[1,1024,1024]{2,1,0:T(8,128)(2,1)S(1)} %copy-done, bf16[1,256,1024]{2,1,0:T(8,128)(2,1)} %param.7, pred[256]{0:T(512)(128)(4,1)S(1)} %fusion.35), kind=kOutput, calls=%fused_computation.14 | convolution fusion | flops 542638080 | bytes 3670272 | tf_op jit(solution)/shard_map/dot_general | solution.py:24
  20.5 0.0 copy-start.2
  20.5 0.8 copy-done.2
  21.3 0.0 copy-done.1
  21.3 2.1 %convert_bitcast_fusion = bf16[1024,1024]{0,1:T(8,128)(2,1)} fusion(bf16[256,1024]{1,0:T(8,128)(2,1)S(1)} %fusion.13, bf16[1,256,1024]{2,1,0:T(8,128)(2,1)S(1)} %copy-done.1), kind=kOutput, calls=%fused_computation.4 | convolution fusion | flops 537919488 | bytes 3145728 | tf_op jit(solution)/shard_map/dot_general | solution.py:32
  23.4 3.9 %copy.23 = bf16[1024,1024]{1,0:T(8,128)(2,1)} copy(bf16[1024,1024]{0,1:T(8,128)(2,1)} %convert_bitcast_fusion) | data formatting | bytes 4194304
  27.3 0.0 copy-start.3
  27.3 0.0 copy-start.4
  27.3 0.0 reduce-scatter.4.cloned.1.call-update
  27.4 0.9 copy-done.3
  28.3 0.2 copy.17
  28.5 0.0 copy-done.4
  28.5 0.2 copy.18
  28.7 2.0 %copy.19 = f32[1,64,1024]{1,2,0:T(8,128)} copy(f32[1,64,1024]{2,1,0:T(8,128)} %param.12) | data formatting | bytes 524288 | tf_op args[5]
  30.6 2.6 %fusion.7 = bf16[1,256,1024]{2,1,0:T(8,128)(2,1)} fusion(bf16[256,1024]{1,0:T(8,128)(2,1)} %copy-done.2, bf16[1,1024,1024]{2,1,0:T(8,128)(2,1)S(1)} %copy-done), kind=kOutput, calls=%fused_computation.10 | convolution fusion | flops 537133056 | bytes 3145728 | tf_op jit(solution)/shard_map/dot_general | solution.py:28
  33.2 93.3 %reduce-scatter.4.cloned.1.call-done = bf16[64,1024]{1,0:T(8,128)(2,1)} async-done(((bf16[1024,1024]{1,0:T(8,128)(2,1)}), bf16[64,1024]{1,0:T(8,128)(2,1)}) %reduce-scatter.4.cloned.1.call-update) | async-done | bytes 131088
  126.5 1.1 copy.24
  127.6 2.6 %fusion.34 = (f32[1,64,1024]{1,2,0:T(8,128)}, f32[1,64,1024]{1,2,0:T(8,128)}, f32[1,64,1024]{1,2,0:T(8,128)}) fusion(bf16[64,1024]{0,1:T(8,128)(2,1)S(1)} %copy.24, f32[1,64,1024]{1,2,0:T(8,128)} %copy.19, f32[1,64,1024]{1,2,0:T(8,128)S(1)} %copy.18, f32[1,64,1024]{1,2,0:T(8,128)S(1)} %copy.17), kind=kLoop, calls=%fused_computation.36 | loop fusion | flops 1114112 | bytes 1703936 | tf_op jit(solution)/shard_map/broadcast_in_dim | solution.py:44
  130.3 1.9 %copy.20 = f32[1,64,1024]{2,1,0:T(8,128)} copy(f32[1,64,1024]{1,2,0:T(8,128)} %get-tuple-element.13) | data formatting | bytes 524288
  132.2 1.9 %copy.21 = f32[1,64,1024]{2,1,0:T(8,128)} copy(f32[1,64,1024]{1,2,0:T(8,128)} %get-tuple-element.14) | data formatting | bytes 524288
  134.1 1.9 %copy.22 = f32[1,64,1024]{2,1,0:T(8,128)} copy(f32[1,64,1024]{1,2,0:T(8,128)} %get-tuple-element.12) | data formatting | bytes 524288
Async XLA Ops:
  7.2 10.9 %copy-start = (bf16[1,1024,1024]{2,1,0:T(8,128)(2,1)S(1)}, bf16[1,1024,1024]{2,1,0:T(8,128)(2,1)}, u32[]{:S(2)}) copy-start(bf16[1,1024,1024]{2,1,0:T(8,128)(2,1)} %param.9) | copy-start | bytes 6291460
  7.2 119.4 %reduce-scatter.4.cloned.1.call-start = ((), (), s32[]{:S(2)}) async-start(), calls=%async_computation.1 | async-start | bytes 2228224
  7.2 10.8 %collective-permute-start = (bf16[1,256,1024]{2,1,0:T(8,128)(2,1)}, bf16[1,256,1024]{2,1,0:T(8,128)(2,1)S(1)}, u32[]{:S(2)}, u32[]{:S(2)}) collective-permute-start(bf16[1,256,1024]{2,1,0:T(8,128)(2,1)} %param.8), channel_id=1, source_target_pairs={{0,1008},{16,0},{32,16},{48,32},{64,48},{80,64},{96,80},{112,96},{... | collective-permute-start | bytes 1572872 | tf_op jit(solution)/shard_map/ppermute | solution.py:14
  11.7 9.6 %copy-start.1 = (bf16[1,256,1024]{2,1,0:T(8,128)(2,1)S(1)}, bf16[1,256,1024]{2,1,0:T(8,128)(2,1)}, u32[]{:S(2)}) copy-start(bf16[1,256,1024]{2,1,0:T(8,128)(2,1)} %param.7) | copy-start | bytes 1572868
  20.5 0.8 copy-start.2
  27.3 0.9 copy-start.3
  27.3 1.2 copy-start.4
Sparse Core Ops, SparseCore 0:
  27.5 99.0 reduce-scatter.3
where the time goes:
time: 143 us
  waiting for transfers between devices  99.6 us (70%)
  local copies, waits for them, and re-layouts  14.9 us (10%)
  between operations  14.1 us (10%)
  matrix products  7.09 us (5%)
  starting transfers between devices  3.82 us (3%)
  other arithmetic  3.37 us (2%)
    unnamed x2, waiting for transfers between devices  93.3 us
    unnamed x18, local copies, waits for them, and re-layouts  14.9 us
    ppermute x1, waiting for transfers between devices, passed_along(): return lax.ppermute(x, axis, [(i, (i + by) % size) for i in range(size)])  6.31 us
    ppermute x1, starting transfers between devices, passed_along(): return lax.ppermute(x, axis, [(i, (i + by) % size) for i in range(size)])  3.78 us
  transfers between devices with their start and end apart: 2, of which 2 were waited for; matrix products, arithmetic and copies ran while one was open for 4% of the time, Pallas kernels for 0%

commit v1 on v0

v1 whole, which is shorter than its diff:
```python
import math

import jax
import jax.numpy as jnp
from jax import lax
from jax.experimental import pallas as pl
from jax.experimental.pallas import tpu as pltpu
from jax.sharding import Mesh
from jax.sharding import PartitionSpec as P

corr_first = 0.9999734386011124
corr_second = 0.09520785288696
X_LO = 2
PAD = 7


def passed_along(x, axis, by):
    size = lax.axis_size(axis)
    return lax.ppermute(x, axis, [(i, (i + by) % size) for i in range(size)])


def weight_term(up_ref, slope_ref, acts_t_ref, lg_ref, total_ref):
    lg = (up_ref[...].astype(jnp.float32) * slope_ref[...]).astype(jnp.bfloat16)
    lg_ref[...] = lg
    total_ref[...] = jnp.dot(acts_t_ref[...], lg, preferred_element_type=jnp.float32).astype(jnp.bfloat16)


def local(saved, passed, weight, master, moment_one, moment_two, counts):
    acts = saved[0]
    w_section = weight[0]
    rows, width = acts.shape
    columns = lax.axis_size("y")
    owned = width // (X_LO * columns)
    upstream = passed_along(passed, "pipe", -1)[0]

    block = rows // counts.shape[0]
    live = jnp.arange(rows) % block < jnp.repeat(counts, block)
    pre = jnp.dot(acts, w_section, preferred_element_type=jnp.float32)
    _, back = jax.vjp(jax.nn.gelu, pre)
    slope = jnp.where(live[:, None], back(jnp.ones_like(pre))[0], jnp.float32(0.0))
    acts_t = acts.T.reshape(X_LO, columns, owned, rows).transpose(1, 0, 2, 3).reshape(columns, X_LO * owned, rows)
    acts_t = jnp.pad(acts_t, ((0, 0), (0, PAD), (0, 0))).reshape(-1, rows)

    vmem = pl.BlockSpec(memory_space=pltpu.VMEM)
    local_grad, total = pl.pallas_call(
        weight_term,
        out_shape=(
            jax.ShapeDtypeStruct((rows, width), jnp.bfloat16),
            jax.ShapeDtypeStruct((acts_t.shape[0], width), jnp.bfloat16),
        ),
        in_specs=[vmem] * 3,
        out_specs=(vmem, vmem),
        compiler_params=pltpu.CompilerParams(vmem_limit_bytes=24 * 1024 * 1024),
        name="weight_term",
    )(upstream, slope, acts_t)

    along_y = lax.optimization_barrier(lax.psum_scatter(total, "y", scatter_dimension=0, tiled=True))
    x_lo = lax.axis_index("x_lo")
    mine = lax.dynamic_slice_in_dim(along_y, x_lo * owned, owned, 0)
    other = lax.dynamic_slice_in_dim(along_y, (1 - x_lo) * owned, owned, 0)
    summed = mine.astype(jnp.float32) + passed_along(other, "x_lo", 1).astype(jnp.float32)

    in_grad = lax.dot_general(
        local_grad, w_section, (((1,), (1,)), ((), ())), preferred_element_type=jnp.float32
    ).astype(jnp.bfloat16)

    grad = summed * (1.0 / math.sqrt(X_LO * columns * rows))
    master_section = master[0]
    first_new = 0.9 * moment_one[0] + 0.1 * grad
    second_new = 0.999 * moment_two[0] + 0.001 * grad * grad
    direction = first_new / corr_first / (jnp.sqrt(second_new / corr_second) + 1e-08)
    master_out = master_section - 0.01 * (direction + 0.1 * master_section)
    return (in_grad[None], master_out[None], first_new[None], second_new[None])


def solution(mesh):
    pipe, dp = mesh.devices.shape
    split = Mesh(mesh.devices.reshape(pipe, X_LO, dp // X_LO), ("pipe", "x_lo", "y"))
    rows = ("x_lo", "y")
    in_specs = (
        P("pipe", rows, None),
        P("pipe", rows, None),
        P("pipe", None, None),
        P("pipe", rows, None),
        P("pipe", rows, None),
        P("pipe", rows, None),
        P(rows),
    )
    out_specs = (
        P("pipe", rows, None),
        P("pipe", rows, None),
        P("pipe", rows, None),
        P("pipe", rows, None),
    )
    return jax.shard_map(local, mesh=split, in_specs=in_specs, out_specs=out_specs, check_vma=False)
```

time: 143 us -> 77.4 us (0.54)
  the two profiles are of different devices: /device:TPU:14 before, /device:TPU:16 now
where the time goes in v1:
time: 77.4 us; the launch traced here: 77 us
  blocking collectives  26.4 us (34%)
  starting transfers between devices  24.8 us (32%)
  waiting for transfers between devices  11.2 us (14%)
  local copies, waits for them, and re-layouts  7.29 us (9%)
  matrix products  3.87 us (5%)
  between operations  1.46 us (2%)
  other arithmetic  1.2 us (2%)
    unnamed x1, blocking collectives  26.4 us
    ppermute x2, starting transfers between devices, passed_along(): return lax.ppermute(x, axis, [(i, (i + by) % size) for i in range(size)])  22.1 us
    ppermute x2, waiting for transfers between devices, passed_along(): return lax.ppermute(x, axis, [(i, (i + by) % size) for i in range(size)])  10.2 us
    unnamed x21, local copies, waits for them, and re-layouts  5.14 us
    unnamed x1, starting transfers between devices  2.69 us
    dot_general x1, matrix products, local(): pre = jnp.dot(acts, w_section, preferred_element_type=jnp.float32)  2.33 us
  transfers between devices with their start and end apart: 3, of which 3 were waited for; matrix products, arithmetic and copies ran while one was open for 11% of the time, Pallas kernels for 0%

profile of v1, /device:TPU:16, one launch (start us, length us, event | category | flops | bytes accessed | tf_op | source)
XLA Modules:
  0.0 77.0 jit_solution(75251796893158151)
XLA Ops:
  0.6 0.0 copy-start
  0.6 0.0 copy-start.7
  0.7 20.1 %collective-permute-start = (bf16[1,256,1024]{2,1,0:T(8,128)(2,1)}, bf16[1,256,1024]{2,1,0:T(8,128)(2,1)S(1)}, u32[]{:S(2)}, u32[]{:S(2)}) collective-permute-start(bf16[1,256,1024]{2,1,0:T(8,128)(2,1)} %param.8), channel_id=1, source_target_pairs={{0,1008},{16,0},{32,16},{48,32},{64,48},{80,64},{96,80},{112,96},{... | collective-permute-start | bytes 1572872 | tf_op jit(solution)/shard_map/ppermute | solution.py:19
  20.7 1.2 %copy.15 = bf16[1,256,1024]{1,2,0:T(8,128)(2,1)S(1)} copy(bf16[1,256,1024]{2,1,0:T(8,128)(2,1)} %param.7) | data formatting | bytes 1048576 | tf_op args[0]
  22.0 0.8 %pad.4 = bf16[8,135,256]{2,1,0:T(8,128)(2,1)} pad(bf16[8,128,256]{2,1,0:T(8,128)(2,1)S(1)} %bitcast.61, bf16[]{:T(256)} %constant.52.clone.1), padding=0_0x0_7x0_0 | pad | bytes 1077250 | tf_op jit(solution)/shard_map/jit(_pad)/pad | solution.py:42
  22.9 1.2 %reshape.41.acts_t_ref = bf16[1080,256]{1,0:T(8,128)(2,1)S(1)} reshape(bf16[8,135,256]{2,1,0:T(8,128)(2,1)} %pad.4) | data formatting | bytes 1105920 | tf_op jit(solution)/shard_map/reshape | solution.py:42
  24.1 0.0 copy-done.7
  24.1 0.1 fusion.26
  24.2 0.0 copy-done
  24.2 2.3 %fusion.17.slope_ref = f32[256,1024]{1,0:T(8,128)S(1)} fusion(bf16[1,1024,1024]{2,1,0:T(8,128)(2,1)S(1)} %copy-done, bf16[1,256,1024]{2,1,0:T(8,128)(2,1)} %param.7, pred[256]{0:T(512)(128)(4,1)S(1)} %fusion.26), kind=kOutput, calls=%fused_computation.14 | convolution fusion | flops 541589504 | bytes 3670272 | tf_op jit(solution)/shard_map/dot_general | solution.py:38
  26.5 6.8 %collective-permute-done = bf16[1,256,1024]{2,1,0:T(8,128)(2,1)S(1)} collective-permute-done((bf16[1,256,1024]{2,1,0:T(8,128)(2,1)}, bf16[1,256,1024]{2,1,0:T(8,128)(2,1)S(1)}, u32[]{:S(2)}, u32[]{:S(2)}) %collective-permute-start) | collective-permute-done | bytes 524320 | tf_op jit(solution)/shard_map/ppermute | solution.py:19
  33.3 0.8 %weight_term.1 = (bf16[256,1024]{1,0:T(8,128)(2,1)S(1)}, bf16[1080,1024]{1,0:T(8,128)(2,1)S(1)}) custom-call(bf16[256,1024]{1,0:T(8,128)(2,1)S(1)} %bitcast.60, f32[256,1024]{1,0:T(8,128)S(1)} %fusion.17.slope_ref, bf16[1080,256]{1,0:T(8,128)(2,1)S(1)} %reshape.41.acts_t_ref), custom_call_target="tpu_custom_call" | custom-call | tf_op jit(solution)/shard_map/weight_term/pallas_call | solution.py:45
  34.1 0.0 copy-start.1
  34.1 1.4 %copy-done.1 = bf16[1080,1024]{1,0:T(8,128)(2,1)} copy-done((bf16[1080,1024]{1,0:T(8,128)(2,1)}, bf16[1080,1024]{1,0:T(8,128)(2,1)S(1)}, u32[]{:S(2)}) %copy-start.1) | copy-done | bytes 2211864
  35.5 0.0 copy-start.2
  35.5 0.8 %copy-done.2 = bf16[256,1024]{1,0:T(8,128)(2,1)} copy-done((bf16[256,1024]{1,0:T(8,128)(2,1)}, bf16[256,1024]{1,0:T(8,128)(2,1)S(1)}, u32[]{:S(2)}) %copy-start.2) | copy-done | bytes 524312
  36.3 0.0 copy-start.3
  36.3 26.4 %fusion = bf16[136,1024]{1,0:T(8,128)(2,1)S(1)} fusion(bf16[1080,1024]{1,0:T(8,128)(2,1)} %copy-done.1), kind=kCustom, calls=%all-reduce-scatter | all-reduce-scatter fusion | flops 1114113 | bytes 2494464
  62.7 2.7 %collective-permute-start.2 = (bf16[7,1024]{1,0:T(8,128)(2,1)S(1)}, bf16[7,1024]{1,0:T(8,128)(2,1)S(1)}, u32[]{:S(2)}, u32[]{:S(2)}) collective-permute-start(bf16[7,1024]{1,0:T(8,128)(2,1)S(1)} %slice), channel_id=1, source_target_pairs={{0,1},{1,2},{2,3},{3,4},{4,5},{5,6},{6,7},{8,9},{9,10},{10,11},{11... | collective-permute-start | bytes 43016
  65.4 1.3 %dynamic-slice.4 = u32[1]{0:T(128)} dynamic-slice(u32[1024]{0:T(1024)} %constant.79, u32[]{:S(6)} %partition-id.4), dynamic_slice_sizes={1} | dynamic-slice | bytes 12
  67.3 1.0 %collective-permute-done.2 = bf16[7,1024]{1,0:T(8,128)(2,1)S(1)} collective-permute-done((bf16[7,1024]{1,0:T(8,128)(2,1)S(1)}, bf16[7,1024]{1,0:T(8,128)(2,1)S(1)}, u32[]{:S(2)}, u32[]{:S(2)}) %collective-permute-start.2) | collective-permute-done | bytes 14368
  68.3 0.3 concatenate
  68.7 0.0 copy-start.4
  68.7 0.0 copy-start.5
  68.7 0.0 copy-start.6
  68.7 0.1 constant_dynamic-slice_fusion
  68.8 2.1 %collective-permute-start.1 = (bf16[64,1024]{1,0:T(8,128)(2,1)S(1)}, bf16[64,1024]{1,0:T(8,128)(2,1)S(1)}, u32[]{:S(2)}, u32[]{:S(2)}) collective-permute-start(bf16[64,1024]{1,0:T(8,128)(2,1)S(1)} %constant_dynamic-slice_fusion.1), channel_id=1, source_target_pairs={{0,8},{8,0},{1,9},{9,1},{2,10},{10,2},{3,11},{11,3},{4,12},{12,4},... | collective-permute-start | bytes 393224 | tf_op jit(solution)/shard_map/ppermute | solution.py:19
  70.9 0.0 copy-done.3
  70.9 1.5 %fusion.8 = bf16[1,256,1024]{2,1,0:T(8,128)(2,1)} fusion(bf16[256,1024]{1,0:T(8,128)(2,1)S(1)} %copy-done.3, bf16[1,1024,1024]{2,1,0:T(8,128)(2,1)S(1)} %copy-done), kind=kOutput, calls=%fused_computation.7 | convolution fusion | flops 537133056 | bytes 3145728 | tf_op jit(solution)/shard_map/dot_general | solution.py:63
  72.5 3.4 %collective-permute-done.1 = bf16[64,1024]{1,0:T(8,128)(2,1)S(1)} collective-permute-done((bf16[64,1024]{1,0:T(8,128)(2,1)S(1)}, bf16[64,1024]{1,0:T(8,128)(2,1)S(1)}, u32[]{:S(2)}, u32[]{:S(2)}) %collective-permute-start.1) | collective-permute-done | bytes 131104 | tf_op jit(solution)/shard_map/ppermute | solution.py:19
  75.8 0.0 copy-done.4
  75.8 0.0 copy-done.5
  75.8 0.0 copy-done.6
  75.8 1.1 %fusion.25 = (f32[1,64,1024]{2,1,0:T(8,128)}, f32[1,64,1024]{2,1,0:T(8,128)}, f32[1,64,1024]{2,1,0:T(8,128)}) fusion(bf16[64,1024]{1,0:T(8,128)(2,1)S(1)} %collective-permute-done.1, bf16[135,1024]{1,0:T(8,128)(2,1)S(1)} %constant_dynamic-slice_fusion, s32[]{:T(128)S(6)} %select_n.23, f32[1,64,1024]{2,1,0:T(8,128)S(1)} %copy-done.4, ...), kind=kLoop, calls=%fused_computation.25 | loop fusion | flops 1245184 | bytes 1835012 | tf_op jit(solution)/shard_map/broadcast_in_dim | solution.py:73
  (3 shorter events, 0.1 us)
Async XLA Ops:
  0.6 23.6 %copy-start = (bf16[1,1024,1024]{2,1,0:T(8,128)(2,1)S(1)}, bf16[1,1024,1024]{2,1,0:T(8,128)(2,1)}, u32[]{:S(2)}) copy-start(bf16[1,1024,1024]{2,1,0:T(8,128)(2,1)} %param.9) | copy-start | bytes 6291460
  0.6 23.5 %copy-start.7 = (s32[2]{0:T(128)S(1)}, s32[2]{0:T(128)}, u32[]{:S(2)}) copy-start(s32[2]{0:T(128)} %param.13) | copy-start | bytes 28
  0.7 32.7 %collective-permute-start = (bf16[1,256,1024]{2,1,0:T(8,128)(2,1)}, bf16[1,256,1024]{2,1,0:T(8,128)(2,1)S(1)}, u32[]{:S(2)}, u32[]{:S(2)}) collective-permute-start(bf16[1,256,1024]{2,1,0:T(8,128)(2,1)} %param.8), channel_id=1, source_target_pairs={{0,1008},{16,0},{32,16},{48,32},{64,48},{80,64},{96,80},{112,96},{... | collective-permute-start | bytes 1572872 | tf_op jit(solution)/shard_map/ppermute | solution.py:19
  34.1 1.4 %copy-start.1 = (bf16[1080,1024]{1,0:T(8,128)(2,1)}, bf16[1080,1024]{1,0:T(8,128)(2,1)S(1)}, u32[]{:S(2)}) copy-start(bf16[1080,1024]{1,0:T(8,128)(2,1)S(1)} %get-tuple-element.7) | copy-start | bytes 6635524
  35.5 0.8 %copy-start.2 = (bf16[256,1024]{1,0:T(8,128)(2,1)}, bf16[256,1024]{1,0:T(8,128)(2,1)S(1)}, u32[]{:S(2)}) copy-start(bf16[256,1024]{1,0:T(8,128)(2,1)S(1)} %get-tuple-element.6) | copy-start | bytes 1572868
  36.3 34.6 %copy-start.3 = (bf16[256,1024]{1,0:T(8,128)(2,1)S(1)}, bf16[256,1024]{1,0:T(8,128)(2,1)}, u32[]{:S(2)}) copy-start(bf16[256,1024]{1,0:T(8,128)(2,1)} %copy-done.2) | copy-start | bytes 1572868
  62.7 5.6 %collective-permute-start.2 = (bf16[7,1024]{1,0:T(8,128)(2,1)S(1)}, bf16[7,1024]{1,0:T(8,128)(2,1)S(1)}, u32[]{:S(2)}, u32[]{:S(2)}) collective-permute-start(bf16[7,1024]{1,0:T(8,128)(2,1)S(1)} %slice), channel_id=1, source_target_pairs={{0,1},{1,2},{2,3},{3,4},{4,5},{5,6},{6,7},{8,9},{9,10},{10,11},{11... | collective-permute-start | bytes 43016
  68.7 7.2 %copy-start.4 = (f32[1,64,1024]{2,1,0:T(8,128)S(1)}, f32[1,64,1024]{2,1,0:T(8,128)}, u32[]{:S(2)}) copy-start(f32[1,64,1024]{2,1,0:T(8,128)} %param.12) | copy-start | bytes 786436
  68.7 7.2 %copy-start.5 = (f32[1,64,1024]{2,1,0:T(8,128)S(1)}, f32[1,64,1024]{2,1,0:T(8,128)}, u32[]{:S(2)}) copy-start(f32[1,64,1024]{2,1,0:T(8,128)} %param.11) | copy-start | bytes 786436
  68.7 7.1 %copy-start.6 = (f32[1,64,1024]{2,1,0:T(8,128)S(1)}, f32[1,64,1024]{2,1,0:T(8,128)}, u32[]{:S(2)}) copy-start(f32[1,64,1024]{2,1,0:T(8,128)} %param.10) | copy-start | bytes 786436
  68.8 7.0 %collective-permute-start.1 = (bf16[64,1024]{1,0:T(8,128)(2,1)S(1)}, bf16[64,1024]{1,0:T(8,128)(2,1)S(1)}, u32[]{:S(2)}, u32[]{:S(2)}) collective-permute-start(bf16[64,1024]{1,0:T(8,128)(2,1)S(1)} %constant_dynamic-slice_fusion.1), channel_id=1, source_target_pairs={{0,8},{8,0},{1,9},{9,1},{2,10},{10,2},{3,11},{11,3},{4,12},{12,4},... | collective-permute-start | bytes 393224 | tf_op jit(solution)/shard_map/ppermute | solution.py:19

commit v2 on v1

--- a/solution.py
+++ b/solution.py
@@ -8,15 +8,12 @@
 from jax.sharding import Mesh
 from jax.sharding import PartitionSpec as P
 
+
 corr_first = 0.9999734386011124
 corr_second = 0.09520785288696
 X_LO = 2
 PAD = 7
-
-
-def passed_along(x, axis, by):
-    size = lax.axis_size(axis)
-    return lax.ppermute(x, axis, [(i, (i + by) % size) for i in range(size)])
+VMEM = pl.BlockSpec(memory_space=pltpu.VMEM)
 
 
 def weight_term(up_ref, slope_ref, acts_t_ref, lg_ref, total_ref):
@@ -25,13 +22,51 @@
     total_ref[...] = jnp.dot(acts_t_ref[...], lg, preferred_element_type=jnp.float32).astype(jnp.bfloat16)
 
 
+def input_term(lg_ref, w_ref, in_grad_ref):
+    in_grad_ref[...] = lax.dot_general(
+        lg_ref[...], w_ref[...], (((1,), (1,)), ((), ())), preferred_element_type=jnp.float32
+    ).astype(jnp.bfloat16)
+
+
+def gradients(upstream, slope, acts_t, w_section):
+    rows, width = upstream.shape
+    owned = width // (X_LO * lax.axis_size("y"))
+    local_grad, total = pl.pallas_call(
+        weight_term,
+        out_shape=(
+            jax.ShapeDtypeStruct((rows, width), jnp.bfloat16),
+            jax.ShapeDtypeStruct((acts_t.shape[0], width), jnp.bfloat16),
+        ),
+        in_specs=[VMEM] * 3,
+        out_specs=(VMEM, VMEM),
+        compiler_params=pltpu.CompilerParams(vmem_limit_bytes=24 * 1024 * 1024),
+        name="weight_term",
+    )(upstream, slope, acts_t)
+    along_y = lax.optimization_barrier(lax.psum_scatter(total, "y", scatter_dimension=0, tiled=True))
+    x_lo = lax.axis_index("x_lo")
+    mine = lax.dynamic_slice_in_dim(along_y, x_lo * owned, owned, 0)
+    other = lax.dynamic_slice_in_dim(along_y, (1 - x_lo) * owned, owned, 0)
+    swapped = lax.ppermute(other, "x_lo", [(0, 1), (1, 0)])
+    in_grad = pl.pallas_call(
+        input_term,
+        out_shape=jax.ShapeDtypeStruct((rows, width), jnp.bfloat16),
+        in_specs=[VMEM] * 2,
+        out_specs=VMEM,
+        cost_estimate=pl.CostEstimate(flops=2 * rows * width * width, bytes_accessed=3 << 20, transcendentals=0),
+        compiler_params=pltpu.CompilerParams(vmem_limit_bytes=24 * 1024 * 1024),
+        name="input_term",
+    )(local_grad, w_section)
+    return in_grad, mine.astype(jnp.float32) + swapped.astype(jnp.float32)
+
+
 def local(saved, passed, weight, master, moment_one, moment_two, counts):
     acts = saved[0]
     w_section = weight[0]
     rows, width = acts.shape
-    columns = lax.axis_size("y")
+    sections, columns = lax.axis_size("pipe"), lax.axis_size("y")
     owned = width // (X_LO * columns)
-    upstream = passed_along(passed, "pipe", -1)[0]
+    near = lax.ppermute(passed[0], "pipe", [(s, s - 1) for s in range(1, sections, 2)])
+    far = lax.ppermute(passed[0], "pipe", [(s, (s - 1) % sections) for s in range(0, sections, 2)])
 
     block = rows // counts.shape[0]
     live = jnp.arange(rows) % block < jnp.repeat(counts, block)
@@ -41,28 +76,13 @@
     acts_t = acts.T.reshape(X_LO, columns, owned, rows).transpose(1, 0, 2, 3).reshape(columns, X_LO * owned, rows)
     acts_t = jnp.pad(acts_t, ((0, 0), (0, PAD), (0, 0))).reshape(-1, rows)
 
-    vmem = pl.BlockSpec(memory_space=pltpu.VMEM)
-    local_grad, total = pl.pallas_call(
-        weight_term,
-        out_shape=(
-            jax.ShapeDtypeStruct((rows, width), jnp.bfloat16),
-            jax.ShapeDtypeStruct((acts_t.shape[0], width), jnp.bfloat16),
-        ),
-        in_specs=[vmem] * 3,
-        out_specs=(vmem, vmem),
-        compiler_params=pltpu.CompilerParams(vmem_limit_bytes=24 * 1024 * 1024),
-        name="weight_term",
-    )(upstream, slope, acts_t)
-
-    along_y = lax.optimization_barrier(lax.psum_scatter(total, "y", scatter_dimension=0, tiled=True))
-    x_lo = lax.axis_index("x_lo")
-    mine = lax.dynamic_slice_in_dim(along_y, x_lo * owned, owned, 0)
-    other = lax.dynamic_slice_in_dim(along_y, (1 - x_lo) * owned, owned, 0)
-    summed = mine.astype(jnp.float32) + passed_along(other, "x_lo", 1).astype(jnp.float32)
-
-    in_grad = lax.dot_general(
-        local_grad, w_section, (((1,), (1,)), ((), ())), preferred_element_type=jnp.float32
-    ).astype(jnp.bfloat16)
+    even = lax.axis_index("pipe") % 2 == 0
+    done = lax.cond(
+        even,
+        lambda: gradients(near, slope, acts_t, w_section),
+        lambda: (jnp.zeros((rows, width), jnp.bfloat16), jnp.zeros((owned, width), jnp.float32)),
+    )
+    in_grad, summed = lax.cond(even, lambda: done, lambda: gradients(far, slope, acts_t, w_section))
 
     grad = summed * (1.0 / math.sqrt(X_LO * columns * rows))
     master_section = master[0]

time: 77.4 us -> 83 us (1.072)
  waiting for transfers between devices: 11.2 us -> 2.84 us
  blocking collectives: 26.4 us -> 33.6 us
  Pallas kernels: 0.77 us -> 5.28 us
  starting transfers between devices: 24.8 us -> 26.7 us
  other arithmetic: 1.2 us -> 2.31 us
    cond x0 -> x1, blocking collectives: none -> 33.6 us
    unnamed x1 -> x0, blocking collectives: 26.4 us -> none
    ppermute x2 -> x3, waiting for transfers between devices: 10.2 us -> 1.24 us  [the longest x1 1.23 us: gradients(): swapped = lax.ppermute(other, 'x_lo', [(0, 1), (1, 0)])]
    cond x0 -> x6, local copies, waits for them, and re-layouts: none -> 5.35 us
    pallas_call x1 -> x2, Pallas kernels: 0.77 us -> 5.28 us  [the longest x1 3.13 us: gradients(): pl.pallas_call(input_term, out_shape=jax.ShapeDtypeStruct((rows, width),...]
    unnamed x21 -> x5, local copies, waits for them, and re-layouts: 5.14 us -> 1.26 us
    unnamed x1 -> x0, starting transfers between devices: 2.69 us -> none
    ppermute x2 -> x3, starting transfers between devices: 22.1 us -> 24.6 us  [the longest x1 20.9 us: local(): lax.ppermute(passed[0], 'pipe', [(s, (s - 1) % sections) for s in range(0...]
  transfers between devices with their start and end apart: 3 -> 4, of which waited for: 3 -> 2; matrix products, arithmetic and copies ran while one was open for 11% -> 52% of each run, Pallas kernels for 0% -> 6%
where the time goes in v2:
time: 83 us; the launch traced here: 82.5 us
  blocking collectives  33.6 us (40%)
  starting transfers between devices  26.7 us (32%)
  local copies, waits for them, and re-layouts  6.89 us (8%)
  Pallas kernels  5.28 us (6%)
  matrix products  3.35 us (4%)
  waiting for transfers between devices  2.84 us (3%)
  other arithmetic  2.31 us (3%)
    cond x1, blocking collectives  33.6 us
    ppermute x1, starting transfers between devices, local(): lax.ppermute(passed[0], 'pipe', [(s, (s - 1) % sections) for s in range(0...  20.9 us
    cond x6, local copies, waits for them, and re-layouts  5.35 us
    dot_general x1, matrix products, local(): pre = jnp.dot(acts, w_section, preferred_element_type=jnp.float32)  3.35 us
    pallas_call x1, Pallas kernels, gradients(): pl.pallas_call(input_term, out_shape=jax.ShapeDtypeStruct((rows, width),...  3.13 us
    ppermute x1, starting transfers between devices, gradients(): swapped = lax.ppermute(other, 'x_lo', [(0, 1), (1, 0)])  2.49 us
    broadcast_in_dim x1, other arithmetic, local(): return (in_grad[None], master_out[None], first_new[None], second_new[None])  2.19 us
    pallas_call x1, Pallas kernels, gradients(): pl.pallas_call(weight_term, out_shape=(jax.ShapeDtypeStruct((rows, width)...  2.16 us
  transfers between devices with their start and end apart: 4, of which 2 were waited for; matrix products, arithmetic and copies ran while one was open for 52% of the time, Pallas kernels for 6%

profile of v2, /device:TPU:16, one launch (start us, length us, event | category | flops | bytes accessed | tf_op | source)
XLA Modules:
  0.0 82.5 jit_solution(106721232290771205)
XLA Ops:
  0.6 0.0 copy-start.2
  0.6 0.0 copy-start
  0.7 20.9 %collective-permute-start.4 = (bf16[256,1024]{1,0:T(8,128)(2,1)}, bf16[256,1024]{1,0:T(8,128)(2,1)}, u32[]{:S(2)}, u32[]{:S(2)}) collective-permute-start(bf16[256,1024]{1,0:T(8,128)(2,1)} %bitcast.60), channel_id=1, source_target_pairs={{0,1008},{32,16},{64,48},{96,80},{128,112},{160,144},{192,176},{22... | collective-permute-start | bytes 1572872 | tf_op jit(solution)/shard_map/ppermute | solution.py:69
  21.5 1.3 %collective-permute-start.5 = (bf16[256,1024]{1,0:T(8,128)(2,1)}, bf16[256,1024]{1,0:T(8,128)(2,1)}, u32[]{:S(2)}, u32[]{:S(2)}) collective-permute-start(bf16[256,1024]{1,0:T(8,128)(2,1)} %bitcast.61), channel_id=1, source_target_pairs={{16,0},{48,32},{80,64},{112,96},{144,128},{176,160},{208,192},{240... | collective-permute-start | bytes 1572872 | tf_op jit(solution)/shard_map/ppermute | solution.py:68
  22.8 1.2 %copy.15 = bf16[1,256,1024]{1,2,0:T(8,128)(2,1)S(1)} copy(bf16[1,256,1024]{2,1,0:T(8,128)(2,1)} %param.11) | data formatting | bytes 1048576 | tf_op args[0]
  24.2 0.2 reshape.41
  24.4 0.0 copy-done.2
  24.4 0.1 fusion.18
  24.4 0.0 copy-done
  24.4 3.3 %fusion.8 = f32[256,1024]{1,0:T(8,128)} fusion(bf16[1,256,1024]{2,1,0:T(8,128)(2,1)} %param.11, pred[256]{0:T(512)(128)(4,1)S(1)} %fusion.18, bf16[1,1024,1024]{2,1,0:T(8,128)(2,1)S(1)} %copy-done), kind=kOutput, calls=%fused_computation.14 | convolution fusion | flops 541589504 | bytes 3670272 | tf_op jit(solution)/shard_map/dot_general | solution.py:73
  27.8 0.0 collective-permute-done.5
  27.8 52.5 %conditional.2 = (bf16[256,1024]{1,0:T(8,128)(2,1)}, f32[64,1024]{1,0:T(8,128)S(1)}) conditional(s32[]{:T(128)} %convert_element_type.18, () %tuple.26, (bf16[256,1024]{1,0:T(8,128)(2,1)}, f32[256,1024]{1,0:T(8,128)}, bf16[1080,256]{1,0:T(8,128)(2,1)S(1)}, bf16[1024,1024]{1,0:T(8,128)(2,1)S(1)}) %tuple.37), branch_computations={%region_0.1_spmd, %region_1.3_spmd} | conditional | flops 538181632 | bytes 16564532 | solution.py:80
  27.8 0.0 copy-start.1
  27.8 1.3 %copy-done.1 = bf16[1024,1024]{1,0:T(8,128)(2,1)} copy-done((bf16[1024,1024]{1,0:T(8,128)(2,1)}, bf16[1024,1024]{1,0:T(8,128)(2,1)S(1)}, u32[]{:S(2)}) %copy-start.1) | copy-done | bytes 2097176 | tf_op jit(solution)/shard_map/cond
  29.1 2.2 %weight_term.2 = (bf16[256,1024]{1,0:T(8,128)(2,1)S(1)}, bf16[1080,1024]{1,0:T(8,128)(2,1)S(1)}) custom-call(bf16[256,1024]{1,0:T(8,128)(2,1)} %get-tuple-element.23.up_ref, f32[256,1024]{1,0:T(8,128)} %get-tuple-element.24.slope_ref, bf16[1080,256]{1,0:T(8,128)(2,1)S(1)} %get-tuple-element.25.acts_t_ref), custom_call_target="tpu_custom_call" | custom-call | tf_op jit(solution)/shard_map/cond/branch_1_fun/weight_term/pallas_call | solution.py:34
  31.3 33.6 %fusion = bf16[136,1024]{1,0:T(8,128)(2,1)} fusion(bf16[1080,1024]{1,0:T(8,128)(2,1)S(1)} %get-tuple-element.28), kind=kCustom, calls=%all-reduce-scatter | all-reduce-scatter fusion | flops 1114113 | bytes 2494464 | tf_op jit(solution)/shard_map/cond
  64.9 0.7 slice
  65.6 2.1 %collective-permute-start.1 = (bf16[7,1024]{1,0:T(8,128)(2,1)S(1)}, bf16[7,1024]{1,0:T(8,128)(2,1)S(1)}, u32[]{:S(2)}, u32[]{:S(2)}) collective-permute-start(bf16[7,1024]{1,0:T(8,128)(2,1)S(1)} %slice), channel_id=1, source_target_pairs={{0,1},{1,2},{2,3},{3,4},{4,5},{5,6},{6,7},{8,9},{9,10},{10,11},{11... | collective-permute-start | bytes 43016 | tf_op jit(solution)/shard_map/cond
  67.7 1.3 %dynamic-slice.6 = u32[1]{0:T(128)} dynamic-slice(u32[1024]{0:T(1024)} %constant.117, u32[]{:S(6)} %partition-id.9), dynamic_slice_sizes={1} | dynamic-slice | bytes 12 | tf_op jit(solution)/shard_map/cond
  69.7 1.6 %collective-permute-done.1 = bf16[7,1024]{1,0:T(8,128)(2,1)S(1)} collective-permute-done((bf16[7,1024]{1,0:T(8,128)(2,1)S(1)}, bf16[7,1024]{1,0:T(8,128)(2,1)S(1)}, u32[]{:S(2)}, u32[]{:S(2)}) %collective-permute-start.1) | collective-permute-done | bytes 14368 | tf_op jit(solution)/shard_map/cond
  71.3 1.9 %concatenate = bf16[143,1024]{1,0:T(8,128)(2,1)S(1)} concatenate(bf16[7,1024]{1,0:T(8,128)(2,1)S(1)} %collective-permute-done.1, bf16[136,1024]{1,0:T(8,128)(2,1)} %fusion), dimensions={0} | concatenate | bytes 585728 | tf_op jit(solution)/shard_map/cond
  73.2 0.1 constant_dynamic-slice_fusion
  73.3 2.5 %collective-permute-start = (bf16[64,1024]{1,0:T(8,128)(2,1)S(1)}, bf16[64,1024]{1,0:T(8,128)(2,1)S(1)}, u32[]{:S(2)}, u32[]{:S(2)}) collective-permute-start(bf16[64,1024]{1,0:T(8,128)(2,1)S(1)} %constant_dynamic-slice_fusion.1), channel_id=1, source_target_pairs={{0,8},{8,0},{1,9},{9,1},{2,10},{10,2},{3,11},{11,3},{4,12},{12,4},... | collective-permute-start | bytes 393224 | tf_op jit(solution)/shard_map/cond/branch_1_fun/ppermute | solution.py:49
  75.8 3.1 %input_term.2 = bf16[256,1024]{1,0:T(8,128)(2,1)} custom-call(bf16[256,1024]{1,0:T(8,128)(2,1)S(1)} %get-tuple-element.26.lg_ref, bf16[1024,1024]{1,0:T(8,128)(2,1)} %copy-done.1), custom_call_target="tpu_custom_call" | custom-call | flops 536870912 | bytes 3145728 | tf_op jit(solution)/shard_map/cond/branch_1_fun/input_term/pallas_call | solution.py:50
  79.0 1.2 %collective-permute-done = bf16[64,1024]{1,0:T(8,128)(2,1)S(1)} collective-permute-done((bf16[64,1024]{1,0:T(8,128)(2,1)S(1)}, bf16[64,1024]{1,0:T(8,128)(2,1)S(1)}, u32[]{:S(2)}, u32[]{:S(2)}) %collective-permute-start) | collective-permute-done | bytes 131104 | tf_op jit(solution)/shard_map/cond/branch_1_fun/ppermute | solution.py:49
  80.3 0.0 collective-permute-done.4
  80.3 2.2 %fusion.17 = (f32[1,64,1024]{2,1,0:T(8,128)}, f32[1,64,1024]{2,1,0:T(8,128)}, f32[1,64,1024]{2,1,0:T(8,128)}) fusion(f32[64,1024]{1,0:T(8,128)S(1)} %get-tuple-element.44, f32[1,64,1024]{2,1,0:T(8,128)} %param.16, f32[1,64,1024]{2,1,0:T(8,128)} %param.15, f32[1,64,1024]{2,1,0:T(8,128)} %param.14), kind=kLoop, calls=%fused_computation.25 | loop fusion | flops 1048576 | bytes 1835008 | tf_op jit(solution)/shard_map/broadcast_in_dim | solution.py:93
  (5 shorter events, 0.2 us)
Async XLA Ops:
  0.6 23.7 %copy-start.2 = (s32[2]{0:T(128)S(1)}, s32[2]{0:T(128)}, u32[]{:S(2)}) copy-start(s32[2]{0:T(128)} %param.17) | copy-start | bytes 28
  0.6 23.8 %copy-start = (bf16[1,1024,1024]{2,1,0:T(8,128)(2,1)S(1)}, bf16[1,1024,1024]{2,1,0:T(8,128)(2,1)}, u32[]{:S(2)}) copy-start(bf16[1,1024,1024]{2,1,0:T(8,128)(2,1)} %param.13) | copy-start | bytes 6291460
  0.7 79.6 %collective-permute-start.4 = (bf16[256,1024]{1,0:T(8,128)(2,1)}, bf16[256,1024]{1,0:T(8,128)(2,1)}, u32[]{:S(2)}, u32[]{:S(2)}) collective-permute-start(bf16[256,1024]{1,0:T(8,128)(2,1)} %bitcast.60), channel_id=1, source_target_pairs={{0,1008},{32,16},{64,48},{96,80},{128,112},{160,144},{192,176},{22... | collective-permute-start | bytes 1572872 | tf_op jit(solution)/shard_map/ppermute | solution.py:69
  21.5 6.3 %collective-permute-start.5 = (bf16[256,1024]{1,0:T(8,128)(2,1)}, bf16[256,1024]{1,0:T(8,128)(2,1)}, u32[]{:S(2)}, u32[]{:S(2)}) collective-permute-start(bf16[256,1024]{1,0:T(8,128)(2,1)} %bitcast.61), channel_id=1, source_target_pairs={{16,0},{48,32},{80,64},{112,96},{144,128},{176,160},{208,192},{240... | collective-permute-start | bytes 1572872 | tf_op jit(solution)/shard_map/ppermute | solution.py:68
  27.8 1.3 %copy-start.1 = (bf16[1024,1024]{1,0:T(8,128)(2,1)}, bf16[1024,1024]{1,0:T(8,128)(2,1)S(1)}, u32[]{:S(2)}) copy-start(bf16[1024,1024]{1,0:T(8,128)(2,1)S(1)} %get-tuple-element.27.w_ref) | copy-start | bytes 6291460 | tf_op jit(solution)/shard_map/cond
  65.6 5.6 %collective-permute-start.1 = (bf16[7,1024]{1,0:T(8,128)(2,1)S(1)}, bf16[7,1024]{1,0:T(8,128)(2,1)S(1)}, u32[]{:S(2)}, u32[]{:S(2)}) collective-permute-start(bf16[7,1024]{1,0:T(8,128)(2,1)S(1)} %slice), channel_id=1, source_target_pairs={{0,1},{1,2},{2,3},{3,4},{4,5},{5,6},{6,7},{8,9},{9,10},{10,11},{11... | collective-permute-start | bytes 43016 | tf_op jit(solution)/shard_map/cond
  73.3 6.9 %collective-permute-start = (bf16[64,1024]{1,0:T(8,128)(2,1)S(1)}, bf16[64,1024]{1,0:T(8,128)(2,1)S(1)}, u32[]{:S(2)}, u32[]{:S(2)}) collective-permute-start(bf16[64,1024]{1,0:T(8,128)(2,1)S(1)} %constant_dynamic-slice_fusion.1), channel_id=1, source_target_pairs={{0,8},{8,0},{1,9},{9,1},{2,10},{10,2},{3,11},{11,3},{4,12},{12,4},... | collective-permute-start | bytes 393224 | tf_op jit(solution)/shard_map/cond/branch_1_fun/ppermute | solution.py:49

commit v3 on v2

--- a/solution.py
+++ b/solution.py
@@ -12,8 +12,30 @@
 corr_first = 0.9999734386011124
 corr_second = 0.09520785288696
 X_LO = 2
-PAD = 7
+COLUMNS = 8
+SPACER = 8
 VMEM = pl.BlockSpec(memory_space=pltpu.VMEM)
+
+
+def prepare(counts_ref, acts_ref, w_ref, slope_ref, acts_t_ref):
+    rows, width = acts_ref.shape
+    batches = counts_ref.shape[0]
+    block = rows // batches
+    owned, stride = width // (X_LO * COLUMNS), width // COLUMNS + SPACER
+    acts = acts_ref[...]
+    acts_t = acts.T
+    for y in range(COLUMNS):
+        for x_lo in range(X_LO):
+            to, at = y * stride + x_lo * owned, x_lo * (width // X_LO) + y * owned
+            acts_t_ref[to : to + owned, :] = acts_t[at : at + owned, :]
+        if y < COLUMNS - 1:
+            acts_t_ref[y * stride + X_LO * owned : (y + 1) * stride, :] = jnp.zeros((SPACER, rows), acts.dtype)
+    for b in range(batches):
+        at = slice(b * block, (b + 1) * block)
+        pre = jnp.dot(acts[at, :], w_ref[...], preferred_element_type=jnp.float32)
+        _, back = jax.vjp(jax.nn.gelu, pre)
+        live = lax.broadcasted_iota(jnp.int32, pre.shape, 0) < counts_ref[b]
+        slope_ref[at, :] = jnp.where(live, back(jnp.ones_like(pre))[0], jnp.float32(0.0))
 
 
 def weight_term(up_ref, slope_ref, acts_t_ref, lg_ref, total_ref):
@@ -30,7 +52,7 @@
 
 def gradients(upstream, slope, acts_t, w_section):
     rows, width = upstream.shape
-    owned = width // (X_LO * lax.axis_size("y"))
+    owned = width // (X_LO * COLUMNS)
     local_grad, total = pl.pallas_call(
         weight_term,
         out_shape=(
@@ -43,10 +65,10 @@
         name="weight_term",
     )(upstream, slope, acts_t)
     along_y = lax.optimization_barrier(lax.psum_scatter(total, "y", scatter_dimension=0, tiled=True))
-    x_lo = lax.axis_index("x_lo")
-    mine = lax.dynamic_slice_in_dim(along_y, x_lo * owned, owned, 0)
-    other = lax.dynamic_slice_in_dim(along_y, (1 - x_lo) * owned, owned, 0)
-    swapped = lax.ppermute(other, "x_lo", [(0, 1), (1, 0)])
+    x_lo, y = lax.axis_index("x_lo"), lax.axis_index("y")
+    mine = lax.dynamic_slice_in_dim(along_y, y + x_lo * owned, owned, 0)
+    other = lax.dynamic_slice_in_dim(along_y, y + (1 - x_lo) * owned, owned, 0)
+    swapped = lax.dynamic_index_in_dim(lax.all_gather(other, "x_lo"), 1 - x_lo, 0, keepdims=False)
     in_grad = pl.pallas_call(
         input_term,
         out_shape=jax.ShapeDtypeStruct((rows, width), jnp.bfloat16),
@@ -63,18 +85,22 @@
     acts = saved[0]
     w_section = weight[0]
     rows, width = acts.shape
-    sections, columns = lax.axis_size("pipe"), lax.axis_size("y")
-    owned = width // (X_LO * columns)
+    sections = lax.axis_size("pipe")
+    owned = width // (X_LO * COLUMNS)
     near = lax.ppermute(passed[0], "pipe", [(s, s - 1) for s in range(1, sections, 2)])
     far = lax.ppermute(passed[0], "pipe", [(s, (s - 1) % sections) for s in range(0, sections, 2)])
 
-    block = rows // counts.shape[0]
-    live = jnp.arange(rows) % block < jnp.repeat(counts, block)
-    pre = jnp.dot(acts, w_section, preferred_element_type=jnp.float32)
-    _, back = jax.vjp(jax.nn.gelu, pre)
-    slope = jnp.where(live[:, None], back(jnp.ones_like(pre))[0], jnp.float32(0.0))
-    acts_t = acts.T.reshape(X_LO, columns, owned, rows).transpose(1, 0, 2, 3).reshape(columns, X_LO * owned, rows)
-    acts_t = jnp.pad(acts_t, ((0, 0), (0, PAD), (0, 0))).reshape(-1, rows)
+    slope, acts_t = pl.pallas_call(
+        prepare,
+        out_shape=(
+            jax.ShapeDtypeStruct((rows, width), jnp.float32),
+            jax.ShapeDtypeStruct((width + (COLUMNS - 1) * SPACER, rows), jnp.bfloat16),
+        ),
+        in_specs=[pl.BlockSpec(memory_space=pltpu.SMEM), VMEM, VMEM],
+        out_specs=(VMEM, VMEM),
+        compiler_params=pltpu.CompilerParams(vmem_limit_bytes=24 * 1024 * 1024),
+        name="prepare",
+    )(counts, acts, w_section)
 
     even = lax.axis_index("pipe") % 2 == 0
     done = lax.cond(
@@ -84,7 +110,7 @@
     )
     in_grad, summed = lax.cond(even, lambda: done, lambda: gradients(far, slope, acts_t, w_section))
 
-    grad = summed * (1.0 / math.sqrt(X_LO * columns * rows))
+    grad = summed * (1.0 / math.sqrt(X_LO * COLUMNS * rows))
     master_section = master[0]
     first_new = 0.9 * moment_one[0] + 0.1 * grad
     second_new = 0.999 * moment_two[0] + 0.001 * grad * grad
@@ -94,8 +120,8 @@
 
 
 def solution(mesh):
-    pipe, dp = mesh.devices.shape
-    split = Mesh(mesh.devices.reshape(pipe, X_LO, dp // X_LO), ("pipe", "x_lo", "y"))
+    pipe = mesh.devices.shape[0]
+    split = Mesh(mesh.devices.reshape(pipe, X_LO, COLUMNS), ("pipe", "x_lo", "y"))
     rows = ("x_lo", "y")
     in_specs = (
         P("pipe", rows, None),

time: 83 us -> 80.1 us (0.965)
  Pallas kernels: 5.28 us -> 9.08 us
  matrix products: 3.35 us -> 0 us
  waiting for transfers between devices: 2.84 us -> 0.01 us
  local copies, waits for them, and re-layouts: 6.89 us -> 4.26 us
  blocking collectives: 33.6 us -> 35 us
  starting transfers between devices: 26.7 us -> 27.7 us
    all_gather x0 -> x1, blocking collectives: none -> 5.64 us  [gradients(): lax.all_gather(other, 'x_lo')]
    cond x1, blocking collectives: 33.6 us -> 29.3 us
    pallas_call x0 -> x1, Pallas kernels: none -> 3.78 us  [local(): pl.pallas_call(prepare, out_shape=(jax.ShapeDtypeStruct((rows, width), jn...]
    dot_general x1 -> x0, matrix products: 3.35 us -> none  [local(): pre = jnp.dot(acts, w_section, preferred_element_type=jnp.float32)]
    cond x6, local copies, waits for them, and re-layouts: 5.35 us -> 2.52 us
    ppermute x1 -> x0, starting transfers between devices: 2.49 us -> none  [gradients(): swapped = lax.ppermute(other, 'x_lo', [(0, 1), (1, 0)])]
    ppermute x1, starting transfers between devices: 20.9 us -> 22.8 us  [local(): lax.ppermute(passed[0], 'pipe', [(s, (s - 1) % sections) for s in range(0...]
    cond x1, waiting for transfers between devices: 1.6 us -> 0.01 us
  transfers between devices with their start and end apart: 4 -> 3, of which waited for: 2 -> 0; matrix products, arithmetic and copies ran while one was open for 52% -> 40% of each run, Pallas kernels for 6% -> 11%
where the time goes in v3:
time: 80.1 us; the launch traced here: 79.7 us
  blocking collectives  35 us (44%)
  starting transfers between devices  27.7 us (35%)
  Pallas kernels  9.08 us (11%)
  local copies, waits for them, and re-layouts  4.26 us (5%)
  other arithmetic  2.25 us (3%)
    cond x1, blocking collectives  29.3 us
    ppermute x1, starting transfers between devices, local(): lax.ppermute(passed[0], 'pipe', [(s, (s - 1) % sections) for s in range(0...  22.8 us
    all_gather x1, blocking collectives, gradients(): lax.all_gather(other, 'x_lo')  5.64 us
    pallas_call x1, Pallas kernels, local(): pl.pallas_call(prepare, out_shape=(jax.ShapeDtypeStruct((rows, width), jn...  3.78 us
    cond x1, starting transfers between devices  3.62 us
    pallas_call x1, Pallas kernels, gradients(): pl.pallas_call(input_term, out_shape=jax.ShapeDtypeStruct((rows, width),...  3.13 us
    cond x6, local copies, waits for them, and re-layouts  2.52 us
    broadcast_in_dim x1, other arithmetic, local(): return (in_grad[None], master_out[None], first_new[None], second_new[None])  2.2 us
  transfers between devices with their start and end apart: 3, of which 0 were waited for; matrix products, arithmetic and copies ran while one was open for 40% of the time, Pallas kernels for 11%

profile of v3, /device:TPU:16, one launch (start us, length us, event | category | flops | bytes accessed | tf_op | source)
XLA Modules:
  0.0 79.7 jit_solution(17420662065634842503)
XLA Ops:
  0.6 1.3 %collective-permute-start.3 = (bf16[256,1024]{1,0:T(8,128)(2,1)}, bf16[256,1024]{1,0:T(8,128)(2,1)}, u32[]{:S(2)}, u32[]{:S(2)}) collective-permute-start(bf16[256,1024]{1,0:T(8,128)(2,1)} %bitcast.54), channel_id=1, source_target_pairs={{16,0},{48,32},{80,64},{112,96},{144,128},{176,160},{208,192},{240... | collective-permute-start | bytes 1572872 | tf_op jit(solution)/shard_map/ppermute | solution.py:90
  1.9 22.8 %collective-permute-start.2 = (bf16[256,1024]{1,0:T(8,128)(2,1)}, bf16[256,1024]{1,0:T(8,128)(2,1)}, u32[]{:S(2)}, u32[]{:S(2)}) collective-permute-start(bf16[256,1024]{1,0:T(8,128)(2,1)} %bitcast.55), channel_id=1, source_target_pairs={{0,1008},{32,16},{64,48},{96,80},{128,112},{160,144},{192,176},{22... | collective-permute-start | bytes 1572872 | tf_op jit(solution)/shard_map/ppermute | solution.py:91
  24.8 0.0 copy-start
  24.8 1.0 %copy-done = bf16[1,256,1024]{2,1,0:T(8,128)(2,1)S(1)} copy-done((bf16[1,256,1024]{2,1,0:T(8,128)(2,1)S(1)}, bf16[1,256,1024]{2,1,0:T(8,128)(2,1)}, u32[]{:S(2)}) %copy-start) | copy-done | bytes 524312
  25.8 0.0 copy-start.1
  25.8 0.7 copy-done.1
  26.5 3.8 %prepare.1 = (f32[256,1024]{1,0:T(8,128)}, bf16[1080,256]{1,0:T(8,128)(2,1)S(1)}) custom-call(s32[2]{0:T(128)S(1)} %copy-done.1, bf16[256,1024]{1,0:T(8,128)(2,1)S(1)} %bitcast.48, bf16[1024,1024]{1,0:T(8,128)(2,1)} %bitcast.49), custom_call_target="tpu_custom_call" | custom-call | tf_op jit(solution)/shard_map/prepare/pallas_call | solution.py:93
  30.2 0.0 collective-permute-done.3
  30.2 47.2 %conditional.2 = (bf16[256,1024]{1,0:T(8,128)(2,1)}, f32[64,1024]{1,0:T(8,128)S(1)}) conditional(s32[]{:T(128)} %convert_element_type.22, () %tuple.26, (bf16[256,1024]{1,0:T(8,128)(2,1)}, f32[256,1024]{1,0:T(8,128)}, bf16[1080,256]{1,0:T(8,128)(2,1)S(1)}, bf16[1024,1024]{1,0:T(8,128)(2,1)}) %tuple.36), branch_computations={%region_0.1_spmd, %region_1.3_spmd} | conditional | flops 538181632 | bytes 9159006 | solution.py:106
  30.2 2.2 %weight_term.2 = (bf16[256,1024]{1,0:T(8,128)(2,1)S(1)}, bf16[1080,1024]{1,0:T(8,128)(2,1)S(1)}) custom-call(bf16[256,1024]{1,0:T(8,128)(2,1)} %get-tuple-element.23.up_ref, f32[256,1024]{1,0:T(8,128)} %get-tuple-element.24.slope_ref, bf16[1080,256]{1,0:T(8,128)(2,1)S(1)} %get-tuple-element.25.acts_t_ref), custom_call_target="tpu_custom_call" | custom-call | tf_op jit(solution)/shard_map/cond/branch_1_fun/weight_term/pallas_call | solution.py:56
  32.4 29.3 %fusion = bf16[136,1024]{1,0:T(8,128)(2,1)} fusion(bf16[1080,1024]{1,0:T(8,128)(2,1)S(1)} %get-tuple-element.28), kind=kCustom, calls=%all-reduce-scatter | all-reduce-scatter fusion | flops 1114113 | bytes 2494464 | tf_op jit(solution)/shard_map/cond
  61.8 0.0 copy-start.2
  61.8 0.8 slice
  62.6 3.6 %collective-permute-start = (bf16[7,1024]{1,0:T(8,128)(2,1)S(1)}, bf16[7,1024]{1,0:T(8,128)(2,1)S(1)}, u32[]{:S(2)}, u32[]{:S(2)}) collective-permute-start(bf16[7,1024]{1,0:T(8,128)(2,1)S(1)} %slice), channel_id=1, source_target_pairs={{0,1},{1,2},{2,3},{3,4},{4,5},{5,6},{6,7},{8,9},{9,10},{10,11},{11... | collective-permute-start | bytes 43016 | tf_op jit(solution)/shard_map/cond
  66.2 3.1 %input_term.2 = bf16[256,1024]{1,0:T(8,128)(2,1)} custom-call(bf16[256,1024]{1,0:T(8,128)(2,1)S(1)} %get-tuple-element.26.lg_ref, bf16[1024,1024]{1,0:T(8,128)(2,1)} %get-tuple-element.27.w_ref), custom_call_target="tpu_custom_call" | custom-call | flops 536870912 | bytes 3145728 | tf_op jit(solution)/shard_map/cond/branch_1_fun/input_term/pallas_call | solution.py:72
  69.3 1.3 %dynamic-slice.6 = u32[1]{0:T(128)} dynamic-slice(u32[1024]{0:T(1024)} %constant.100, u32[]{:S(6)} %partition-id.9), dynamic_slice_sizes={1} | dynamic-slice | bytes 12 | tf_op jit(solution)/shard_map/cond
  71.2 0.0 collective-permute-done
  71.2 0.0 copy-done.2
  71.3 0.4 concatenate
  71.6 0.1 constant_dynamic-slice_fusion
  71.8 5.6 %all-gather = bf16[128,1024]{1,0:T(8,128)(2,1)S(1)} all-gather(bf16[64,1024]{1,0:T(8,128)(2,1)S(1)} %constant_dynamic-slice_fusion.1), channel_id=2, replica_groups=mesh['pipe'=64,'x_lo'=2,'y'=8] {'x_lo'}, dimensions={0}, use_global_device_ids=true | all-gather | bytes 393216 | tf_op jit(solution)/shard_map/cond/branch_1_fun/all_gather | solution.py:71
  77.4 0.1 convert_add_fusion
  77.5 0.0 collective-permute-done.2
  77.5 2.2 %fusion.6 = (f32[1,64,1024]{2,1,0:T(8,128)}, f32[1,64,1024]{2,1,0:T(8,128)}, f32[1,64,1024]{2,1,0:T(8,128)}) fusion(f32[64,1024]{1,0:T(8,128)S(1)} %get-tuple-element.48, f32[1,64,1024]{2,1,0:T(8,128)} %param.16, f32[1,64,1024]{2,1,0:T(8,128)} %param.15, f32[1,64,1024]{2,1,0:T(8,128)} %param.14), kind=kLoop, calls=%fused_computation.14 | loop fusion | flops 1048576 | bytes 1835008 | tf_op jit(solution)/shard_map/broadcast_in_dim | solution.py:119
  (2 shorter events, 0.1 us)
Async XLA Ops:
  0.6 29.6 %collective-permute-start.3 = (bf16[256,1024]{1,0:T(8,128)(2,1)}, bf16[256,1024]{1,0:T(8,128)(2,1)}, u32[]{:S(2)}, u32[]{:S(2)}) collective-permute-start(bf16[256,1024]{1,0:T(8,128)(2,1)} %bitcast.54), channel_id=1, source_target_pairs={{16,0},{48,32},{80,64},{112,96},{144,128},{176,160},{208,192},{240... | collective-permute-start | bytes 1572872 | tf_op jit(solution)/shard_map/ppermute | solution.py:90
  1.9 75.5 %collective-permute-start.2 = (bf16[256,1024]{1,0:T(8,128)(2,1)}, bf16[256,1024]{1,0:T(8,128)(2,1)}, u32[]{:S(2)}, u32[]{:S(2)}) collective-permute-start(bf16[256,1024]{1,0:T(8,128)(2,1)} %bitcast.55), channel_id=1, source_target_pairs={{0,1008},{32,16},{64,48},{96,80},{128,112},{160,144},{192,176},{22... | collective-permute-start | bytes 1572872 | tf_op jit(solution)/shard_map/ppermute | solution.py:91
  24.8 1.0 %copy-start = (bf16[1,256,1024]{2,1,0:T(8,128)(2,1)S(1)}, bf16[1,256,1024]{2,1,0:T(8,128)(2,1)}, u32[]{:S(2)}) copy-start(bf16[1,256,1024]{2,1,0:T(8,128)(2,1)} %param.11) | copy-start | bytes 1572868
  25.8 0.7 copy-start.1
  61.8 9.5 %copy-start.2 = (bf16[136,1024]{1,0:T(8,128)(2,1)S(1)}, bf16[136,1024]{1,0:T(8,128)(2,1)}, u32[]{:S(2)}) copy-start(bf16[136,1024]{1,0:T(8,128)(2,1)} %fusion) | copy-start | bytes 835588 | tf_op jit(solution)/shard_map/cond
  62.6 8.7 %collective-permute-start = (bf16[7,1024]{1,0:T(8,128)(2,1)S(1)}, bf16[7,1024]{1,0:T(8,128)(2,1)S(1)}, u32[]{:S(2)}, u32[]{:S(2)}) collective-permute-start(bf16[7,1024]{1,0:T(8,128)(2,1)S(1)} %slice), channel_id=1, source_target_pairs={{0,1},{1,2},{2,3},{3,4},{4,5},{5,6},{6,7},{8,9},{9,10},{10,11},{11... | collective-permute-start | bytes 43016 | tf_op jit(solution)/shard_map/cond

commit v4 on v3

v4 whole, which is shorter than its diff:
```python
import math

import jax
import jax.numpy as jnp
from jax import lax
from jax.experimental import pallas as pl
from jax.experimental.pallas import tpu as pltpu
from jax.sharding import Mesh
from jax.sharding import PartitionSpec as P


corr_first = 0.9999734386011124
corr_second = 0.09520785288696
X_LO = 2
COLUMNS = 8
SPACER = 8
VMEM = pl.BlockSpec(memory_space=pltpu.VMEM)


def prepare(counts_ref, acts_ref, w_ref, slope_ref, acts_t_ref):
    rows, width = acts_ref.shape
    batches = counts_ref.shape[0]
    block = rows // batches
    owned, stride = width // (X_LO * COLUMNS), width // COLUMNS + SPACER
    acts = acts_ref[...]
    acts_t = acts.T
    for y in range(COLUMNS):
        for x_lo in range(X_LO):
            to, at = y * stride + x_lo * owned, x_lo * (width // X_LO) + y * owned
            acts_t_ref[to : to + owned, :] = acts_t[at : at + owned, :]
        if y < COLUMNS - 1:
            acts_t_ref[y * stride + X_LO * owned : (y + 1) * stride, :] = jnp.zeros((SPACER, rows), acts.dtype)
    for b in range(batches):
        at = slice(b * block, (b + 1) * block)
        pre = jnp.dot(acts[at, :], w_ref[...], preferred_element_type=jnp.float32)
        _, back = jax.vjp(jax.nn.gelu, pre)
        live = lax.broadcasted_iota(jnp.int32, pre.shape, 0) < counts_ref[b]
        slope_ref[at, :] = jnp.where(live, back(jnp.ones_like(pre))[0], jnp.float32(0.0))


def weight_term(up_ref, slope_ref, acts_t_ref, lg_ref, total_ref):
    lg = (up_ref[...].astype(jnp.float32) * slope_ref[...]).astype(jnp.bfloat16)
    lg_ref[...] = lg
    total_ref[...] = jnp.dot(acts_t_ref[...], lg, preferred_element_type=jnp.float32).astype(jnp.bfloat16)


def input_term(lg_ref, w_ref, in_grad_ref):
    in_grad_ref[...] = lax.dot_general(
        lg_ref[...], w_ref[...], (((1,), (1,)), ((), ())), preferred_element_type=jnp.float32
    ).astype(jnp.bfloat16)


def unwritten(ref):
    del ref


def blank(shape, dtype):
    return pl.pallas_call(
        unwritten, out_shape=jax.ShapeDtypeStruct(shape, dtype), out_specs=pl.BlockSpec(memory_space=pl.ANY), name="blank"
    )()


def prepared(counts, acts, w_section):
    rows, width = acts.shape
    return pl.pallas_call(
        prepare,
        out_shape=(
            jax.ShapeDtypeStruct((rows, width), jnp.float32),
            jax.ShapeDtypeStruct((width + (COLUMNS - 1) * SPACER, rows), jnp.bfloat16),
        ),
        in_specs=[pl.BlockSpec(memory_space=pltpu.SMEM), VMEM, VMEM],
        out_specs=(VMEM, VMEM),
        compiler_params=pltpu.CompilerParams(vmem_limit_bytes=24 * 1024 * 1024),
        name="prepare",
    )(counts, acts, w_section)


def weight_gradient(upstream, slope, acts_t):
    rows, width = upstream.shape
    return pl.pallas_call(
        weight_term,
        out_shape=(
            jax.ShapeDtypeStruct((rows, width), jnp.bfloat16),
            jax.ShapeDtypeStruct((acts_t.shape[0], width), jnp.bfloat16),
        ),
        in_specs=[VMEM] * 3,
        out_specs=(VMEM, VMEM),
        compiler_params=pltpu.CompilerParams(vmem_limit_bytes=24 * 1024 * 1024),
        name="weight_term",
    )(upstream, slope, acts_t)


def input_gradient(local_grad, w_section):
    rows, width = local_grad.shape
    return pl.pallas_call(
        input_term,
        out_shape=jax.ShapeDtypeStruct((rows, width), jnp.bfloat16),
        in_specs=[VMEM] * 2,
        out_specs=VMEM,
        cost_estimate=pl.CostEstimate(flops=2 * rows * width * width, bytes_accessed=3 << 20, transcendentals=0),
        compiler_params=pltpu.CompilerParams(vmem_limit_bytes=24 * 1024 * 1024),
        name="input_term",
    )(local_grad, w_section)


def updated(total, master_section, first, second, slots):
    owned = total.shape[1] // (X_LO * COLUMNS)
    along_y = lax.optimization_barrier(lax.psum_scatter(total, "y", scatter_dimension=0, tiled=True))
    x_lo, y = lax.axis_index("x_lo"), lax.axis_index("y")
    mine = lax.dynamic_slice_in_dim(along_y, y + x_lo * owned, owned, 0)
    other = lax.dynamic_slice_in_dim(along_y, y + (1 - x_lo) * owned, owned, 0)
    swapped = lax.dynamic_index_in_dim(lax.all_gather(other, "x_lo"), 1 - x_lo, 0, keepdims=False)
    summed = mine.astype(jnp.float32) + swapped.astype(jnp.float32)
    grad = summed * (1.0 / math.sqrt(slots))
    first_new = 0.9 * first + 0.1 * grad
    second_new = 0.999 * second + 0.001 * grad * grad
    direction = first_new / corr_first / (jnp.sqrt(second_new / corr_second) + 1e-08)
    master_out = master_section - 0.01 * (direction + 0.1 * master_section)
    return master_out, first_new, second_new


def local(saved, passed, weight, master, moment_one, moment_two, counts):
    acts, w_section, block = saved[0], weight[0], passed[0]
    rows, width = acts.shape
    sections = lax.axis_size("pipe")
    section = lax.axis_index("pipe")
    slots = X_LO * COLUMNS * rows
    parts = (master[0], moment_one[0], moment_two[0])
    padded = width + (COLUMNS - 1) * SPACER

    def chain(upstream, slope, acts_t):
        local_grad, total = weight_gradient(upstream, slope, acts_t)
        new = updated(total, *parts, slots)
        return (input_gradient(local_grad, w_section), *new)

    def first_front(upstream):
        local_grad, total = weight_gradient(upstream, *prepared(counts, acts, w_section))
        return input_gradient(local_grad, w_section), total

    def nothing():
        return (blank((rows, width), jnp.bfloat16), *(blank(p.shape, p.dtype) for p in parts))

    own = lax.ppermute(block, "pipe", [(1, 0)])
    front = lax.cond(
        section == 0,
        first_front,
        lambda _: (blank((rows, width), jnp.bfloat16), blank((padded, width), jnp.bfloat16)),
        own,
    )
    far = lax.ppermute(block, "pipe", [(s, (s - 1) % sections) for s in range(0, sections, 2)])
    near = lax.ppermute(block, "pipe", [(s, s - 1) for s in range(3, sections, 2)])
    slope, acts_t = lax.cond(
        section == 0,
        lambda *_: (blank((rows, width), jnp.float32), blank((padded, rows), jnp.bfloat16)),
        prepared,
        counts,
        acts,
        w_section,
    )
    kind = jnp.where(section == 0, 0, 1 + section % 2)
    even = lax.switch(
        kind,
        (
            lambda: (front[0], *updated(front[1], *parts, slots)),
            lambda: chain(near, slope, acts_t),
            nothing,
        ),
    )
    out = lax.cond(section % 2 == 0, lambda: even, lambda: chain(far, slope, acts_t))
    return tuple(x[None] for x in out)


def solution(mesh):
    pipe = mesh.devices.shape[0]
    split = Mesh(mesh.devices.reshape(pipe, X_LO, COLUMNS), ("pipe", "x_lo", "y"))
    rows = ("x_lo", "y")
    in_specs = (
        P("pipe", rows, None),
        P("pipe", rows, None),
        P("pipe", None, None),
        P("pipe", rows, None),
        P("pipe", rows, None),
        P("pipe", rows, None),
        P(rows),
    )
    out_specs = (
        P("pipe", rows, None),
        P("pipe", rows, None),
        P("pipe", rows, None),
        P("pipe", rows, None),
    )
    return jax.shard_map(local, mesh=split, in_specs=in_specs, out_specs=out_specs, check_vma=False)
```

time: 80.1 us -> 74.9 us (0.935)
  Pallas kernels: 9.08 us -> 6.01 us
  other arithmetic: 2.25 us -> 0.27 us
    pallas_call x3 -> x5, Pallas kernels: 9.08 us -> 6.01 us  [the longest x1 3.11 us: prepared(): pl.pallas_call(prepare, out_shape=(jax.ShapeDtypeStruct((rows, width), jn...]
    broadcast_in_dim x1 -> x0, other arithmetic: 2.2 us -> none  [local(): return (in_grad[None], master_out[None], first_new[None], second_new[None])]
    cond x6, local copies, waits for them, and re-layouts: 2.52 us -> 1.7 us
    unnamed x4 -> x18, local copies, waits for them, and re-layouts: 1.7 us -> 1.83 us
    ppermute x2 -> x3, starting transfers between devices: 24.1 us -> 24.1 us  [the longest x1 22.1 us: local(): lax.ppermute(block, 'pipe', [(s, (s - 1) % sections) for s in range(0, se...]
  transfers between devices with their start and end apart: 3 -> 4, of which waited for: 0 -> 1; matrix products, arithmetic and copies ran while one was open for 40% -> 43% of each run, Pallas kernels for 11% -> 8%
where the time goes in v4:
time: 74.9 us; the launch traced here: 74.5 us
  blocking collectives  35.4 us (47%)
  starting transfers between devices  27.4 us (37%)
  Pallas kernels  6.01 us (8%)
  local copies, waits for them, and re-layouts  3.57 us (5%)
  between operations  0.75 us (1%)
    cond x1, blocking collectives  29.8 us
    ppermute x1, starting transfers between devices, local(): lax.ppermute(block, 'pipe', [(s, (s - 1) % sections) for s in range(0, se...  22.1 us
    all_gather x1, blocking collectives, updated(): lax.all_gather(other, 'x_lo')  5.64 us
    cond x1, starting transfers between devices  3.38 us
    pallas_call x1, Pallas kernels, prepared(): pl.pallas_call(prepare, out_shape=(jax.ShapeDtypeStruct((rows, width), jn...  3.11 us
    pallas_call x1, Pallas kernels, weight_gradient(): pl.pallas_call(weight_term, out_shape=(jax.ShapeDtypeStruct((rows, width)...  2.16 us
    unnamed x18, local copies, waits for them, and re-layouts  1.83 us
    cond x6, local copies, waits for them, and re-layouts  1.7 us
  transfers between devices with their start and end apart: 4, of which 1 were waited for; matrix products, arithmetic and copies ran while one was open for 43% of the time, Pallas kernels for 8%

profile of v4, /device:TPU:16, one launch (start us, length us, event | category | flops | bytes accessed | tf_op | source)
XLA Modules:
  0.0 74.5 jit_solution(14340874226551329903)
XLA Ops:
  0.6 1.3 %collective-permute-start.4 = (bf16[256,1024]{1,0:T(8,128)(2,1)}, bf16[256,1024]{1,0:T(8,128)(2,1)S(1)}, u32[]{:S(2)}, u32[]{:S(2)}) collective-permute-start(bf16[256,1024]{1,0:T(8,128)(2,1)} %bitcast.76), channel_id=1, source_target_pairs={{16,0},{17,1},{18,2},{19,3},{20,4},{21,5},{22,6},{23,7},{24,8},{25... | collective-permute-start | bytes 1572872 | tf_op jit(solution)/shard_map/ppermute | solution.py:143
  1.9 0.7 collective-permute-start.5
  2.6 22.1 %collective-permute-start.3 = (bf16[256,1024]{1,0:T(8,128)(2,1)}, bf16[256,1024]{1,0:T(8,128)(2,1)}, u32[]{:S(2)}, u32[]{:S(2)}) collective-permute-start(bf16[256,1024]{1,0:T(8,128)(2,1)} %bitcast.78), channel_id=1, source_target_pairs={{0,1008},{32,16},{64,48},{96,80},{128,112},{160,144},{192,176},{22... | collective-permute-start | bytes 1572872 | tf_op jit(solution)/shard_map/ppermute | solution.py:150
  24.7 0.0 copy-start.6
  24.7 0.0 copy-start.1
  24.7 0.0 collective-permute-done.4
  24.7 0.8 %copy-done.6 = bf16[1080,256]{1,0:T(8,128)(2,1)} copy-done((bf16[1080,256]{1,0:T(8,128)(2,1)}, bf16[1080,256]{1,0:T(8,128)(2,1)S(1)}, u32[]{:S(2)}) %copy-start.6) | copy-done | bytes 552984
  25.5 0.0 copy-start.3
  25.5 0.0 copy-start.4
  25.5 0.0 copy-start.5
  25.5 6.0 %conditional.5 = (bf16[256,1024]{1,0:T(8,128)(2,1)S(1)}, bf16[1080,1024]{1,0:T(8,128)(2,1)}) conditional(s32[]{:T(128)} %convert_element_type.35, () %tuple.52, (s32[2]{0:T(128)}, bf16[256,1024]{1,0:T(8,128)(2,1)}, bf16[1024,1024]{1,0:T(8,128)(2,1)}, bf16[256,1024]{1,0:T(8,128)(2,1)S(1)}) %tuple.100), branch_computations={%region_2.0_spmd, %region_3.0_spmd} | conditional | flops 536870912 | bytes 11534380 | solution.py:144
  25.5 0.0 copy-start
  25.5 3.1 %prepare.3 = (f32[256,1024]{1,0:T(8,128)S(1)}, bf16[1080,256]{1,0:T(8,128)(2,1)S(1)}) custom-call(s32[2]{0:T(128)} %get-tuple-element.72.counts_ref, bf16[256,1024]{1,0:T(8,128)(2,1)} %get-tuple-element.73.acts_ref, bf16[1024,1024]{1,0:T(8,128)(2,1)} %get-tuple-element.74.w_ref), custom_call_target="tpu_custom_call" | custom-call | tf_op jit(solution)/shard_map/cond/branch_1_fun/prepare/pallas_call | solution.py:65
  28.7 2.2 %weight_term.3 = (bf16[256,1024]{1,0:T(8,128)(2,1)S(1)}, bf16[1080,1024]{1,0:T(8,128)(2,1)}) custom-call(bf16[256,1024]{1,0:T(8,128)(2,1)S(1)} %get-tuple-element.71.up_ref, f32[256,1024]{1,0:T(8,128)S(1)} %get-tuple-element.75.slope_ref, bf16[1080,256]{1,0:T(8,128)(2,1)S(1)} %get-tuple-element.76.acts_t_ref), custom_call_target="tpu_custom_call" | custom-call | tf_op jit(solution)/shard_map/cond/branch_1_fun/weight_term/pallas_call | solution.py:80
  30.8 0.0 copy-done
  30.8 0.7 input_term.3
  31.6 0.0 collective-permute-done.5
  31.6 0.0 copy-done.3
  31.6 0.0 copy-done.4
  31.6 0.0 copy-done.5
  31.6 0.0 copy-done.1
  31.6 41.9 %conditional.6 = (bf16[256,1024]{1,0:T(8,128)(2,1)S(1)}, f32[64,1024]{1,0:T(8,128)S(1)}, f32[64,1024]{1,0:T(8,128)S(1)}, f32[64,1024]{1,0:T(8,128)S(1)}) conditional(s32[]{:T(128)} %clamp.3, (f32[64,1024]{1,0:T(8,128)S(1)}, bf16[1080,1024]{1,0:T(8,128)(2,1)}, f32[64,1024]{1,0:T(8,128)S(1)}, f32[64,1024]{1,0:T(8,128)S(1)}, ...), branch_computations={%region_4.6_spmd, %region_6.8_spmd, %region_8.9_spmd} | conditional | flops 539230208 | bytes 16761254 | solution.py:161
  31.6 29.8 %fusion = bf16[136,1024]{1,0:T(8,128)(2,1)S(1)} fusion(bf16[1080,1024]{1,0:T(8,128)(2,1)} %get-tuple-element.82), kind=kCustom, calls=%all-reduce-scatter | all-reduce-scatter fusion | flops 1114113 | bytes 2494464 | tf_op jit(solution)/shard_map/cond
  61.4 3.4 %collective-permute-start.1 = (bf16[7,1024]{1,0:T(8,128)(2,1)S(1)}, bf16[7,1024]{1,0:T(8,128)(2,1)S(1)}, u32[]{:S(2)}, u32[]{:S(2)}) collective-permute-start(bf16[7,1024]{1,0:T(8,128)(2,1)S(1)} %slice), channel_id=1, source_target_pairs={{0,1},{1,2},{2,3},{3,4},{4,5},{5,6},{6,7},{8,9},{9,10},{10,11},{11... | collective-permute-start | bytes 43016 | tf_op jit(solution)/shard_map/cond
  64.8 1.3 %dynamic-slice.8 = u32[1]{0:T(128)} dynamic-slice(u32[1024]{0:T(1024)} %constant.166, u32[]{:S(6)} %partition-id.15), dynamic_slice_sizes={1} | dynamic-slice | bytes 12 | tf_op jit(solution)/shard_map/cond
  66.7 0.4 collective-permute-done.1
  67.1 0.3 concatenate
  67.4 0.1 constant_dynamic-slice_fusion
  67.6 5.6 %all-gather = bf16[128,1024]{1,0:T(8,128)(2,1)S(1)} all-gather(bf16[64,1024]{1,0:T(8,128)(2,1)S(1)} %constant_dynamic-slice_fusion.1), channel_id=2, replica_groups=mesh['pipe'=64,'x_lo'=2,'y'=8] {'x_lo'}, dimensions={0}, use_global_device_ids=true | all-gather | bytes 393216 | tf_op jit(solution)/shard_map/cond/branch_0_fun/all_gather | solution.py:112
  73.2 0.3 multiply_subtract_fusion
  73.5 0.0 copy-start.9
  73.5 0.0 copy-start.11
  73.5 0.0 copy-start.12
  73.5 0.0 copy-start.13
  73.5 0.0 collective-permute-done.3
  73.5 0.7 copy-done.9
  74.3 0.1 copy-done.11
  74.4 0.1 copy-done.12
  74.4 0.1 copy-done.13
  (6 shorter events, 0.1 us)
Async XLA Ops:
  0.6 24.1 %collective-permute-start.4 = (bf16[256,1024]{1,0:T(8,128)(2,1)}, bf16[256,1024]{1,0:T(8,128)(2,1)S(1)}, u32[]{:S(2)}, u32[]{:S(2)}) collective-permute-start(bf16[256,1024]{1,0:T(8,128)(2,1)} %bitcast.76), channel_id=1, source_target_pairs={{16,0},{17,1},{18,2},{19,3},{20,4},{21,5},{22,6},{23,7},{24,8},{25... | collective-permute-start | bytes 1572872 | tf_op jit(solution)/shard_map/ppermute | solution.py:143
  1.9 29.6 %collective-permute-start.5 = (bf16[256,1024]{1,0:T(8,128)(2,1)}, bf16[256,1024]{1,0:T(8,128)(2,1)S(1)}, u32[]{:S(2)}, u32[]{:S(2)}) collective-permute-start(bf16[256,1024]{1,0:T(8,128)(2,1)} %bitcast.77), channel_id=1, source_target_pairs={{48,32},{80,64},{112,96},{144,128},{176,160},{208,192},{240,224},{... | collective-permute-start | bytes 1572872 | tf_op jit(solution)/shard_map/ppermute | solution.py:151
  2.6 70.9 %collective-permute-start.3 = (bf16[256,1024]{1,0:T(8,128)(2,1)}, bf16[256,1024]{1,0:T(8,128)(2,1)}, u32[]{:S(2)}, u32[]{:S(2)}) collective-permute-start(bf16[256,1024]{1,0:T(8,128)(2,1)} %bitcast.78), channel_id=1, source_target_pairs={{0,1008},{32,16},{64,48},{96,80},{128,112},{160,144},{192,176},{22... | collective-permute-start | bytes 1572872 | tf_op jit(solution)/shard_map/ppermute | solution.py:150
  24.7 0.8 %copy-start.6 = (bf16[1080,256]{1,0:T(8,128)(2,1)}, bf16[1080,256]{1,0:T(8,128)(2,1)S(1)}, u32[]{:S(2)}) copy-start(bf16[1080,256]{1,0:T(8,128)(2,1)S(1)} %get-tuple-element.115) | copy-start | bytes 1658884
  24.7 6.9 %copy-start.1 = (f32[256,1024]{1,0:T(8,128)}, f32[256,1024]{1,0:T(8,128)S(1)}, u32[]{:S(2)}) copy-start(f32[256,1024]{1,0:T(8,128)S(1)} %get-tuple-element.114) | copy-start | bytes 3145732
  25.5 6.0 %copy-start.3 = (f32[1,64,1024]{2,1,0:T(8,128)S(1)}, f32[1,64,1024]{2,1,0:T(8,128)}, u32[]{:S(2)}) copy-start(f32[1,64,1024]{2,1,0:T(8,128)} %param.20) | copy-start | bytes 786436
  25.5 6.1 %copy-start.4 = (f32[1,64,1024]{2,1,0:T(8,128)S(1)}, f32[1,64,1024]{2,1,0:T(8,128)}, u32[]{:S(2)}) copy-start(f32[1,64,1024]{2,1,0:T(8,128)} %param.21) | copy-start | bytes 786436
  25.5 6.1 %copy-start.5 = (f32[1,64,1024]{2,1,0:T(8,128)S(1)}, f32[1,64,1024]{2,1,0:T(8,128)}, u32[]{:S(2)}) copy-start(f32[1,64,1024]{2,1,0:T(8,128)} %param.19) | copy-start | bytes 786436
  25.5 5.3 %copy-start = (bf16[1024,1024]{1,0:T(8,128)(2,1)S(1)}, bf16[1024,1024]{1,0:T(8,128)(2,1)}, u32[]{:S(2)}) copy-start(bf16[1024,1024]{1,0:T(8,128)(2,1)} %get-tuple-element.74.w_ref) | copy-start | bytes 6291460 | tf_op jit(solution)/shard_map/cond
  61.4 5.7 %collective-permute-start.1 = (bf16[7,1024]{1,0:T(8,128)(2,1)S(1)}, bf16[7,1024]{1,0:T(8,128)(2,1)S(1)}, u32[]{:S(2)}, u32[]{:S(2)}) collective-permute-start(bf16[7,1024]{1,0:T(8,128)(2,1)S(1)} %slice), channel_id=1, source_target_pairs={{0,1},{1,2},{2,3},{3,4},{4,5},{5,6},{6,7},{8,9},{9,10},{10,11},{11... | collective-permute-start | bytes 43016 | tf_op jit(solution)/shard_map/cond
  73.5 0.8 %copy-start.9 = (bf16[256,1024]{1,0:T(8,128)(2,1)}, bf16[256,1024]{1,0:T(8,128)(2,1)S(1)}, u32[]{:S(2)}) copy-start(bf16[256,1024]{1,0:T(8,128)(2,1)S(1)} %get-tuple-element.166) | copy-start | bytes 1572868
  73.5 0.9 %copy-start.11 = (f32[64,1024]{1,0:T(8,128)}, f32[64,1024]{1,0:T(8,128)S(1)}, u32[]{:S(2)}) copy-start(f32[64,1024]{1,0:T(8,128)S(1)} %get-tuple-element.167) | copy-start | bytes 786436
  73.5 0.9 %copy-start.12 = (f32[64,1024]{1,0:T(8,128)}, f32[64,1024]{1,0:T(8,128)S(1)}, u32[]{:S(2)}) copy-start(f32[64,1024]{1,0:T(8,128)S(1)} %get-tuple-element.168) | copy-start | bytes 786436
  73.5 1.0 %copy-start.13 = (f32[64,1024]{1,0:T(8,128)}, f32[64,1024]{1,0:T(8,128)S(1)}, u32[]{:S(2)}) copy-start(f32[64,1024]{1,0:T(8,128)S(1)} %get-tuple-element.169) | copy-start | bytes 786436

commit v5 on v4

--- a/solution.py
+++ b/solution.py
@@ -140,6 +140,7 @@
     def nothing():
         return (blank((rows, width), jnp.bfloat16), *(blank(p.shape, p.dtype) for p in parts))
 
+    far = lax.ppermute(block, "pipe", [(s, s - 1) for s in range(2, sections, 2)])
     own = lax.ppermute(block, "pipe", [(1, 0)])
     front = lax.cond(
         section == 0,
@@ -147,7 +148,7 @@
         lambda _: (blank((rows, width), jnp.bfloat16), blank((padded, width), jnp.bfloat16)),
         own,
     )
-    far = lax.ppermute(block, "pipe", [(s, (s - 1) % sections) for s in range(0, sections, 2)])
+    around = lax.ppermute(block, "pipe", [(0, sections - 1)])
     near = lax.ppermute(block, "pipe", [(s, s - 1) for s in range(3, sections, 2)])
     slope, acts_t = lax.cond(
         section == 0,
@@ -157,16 +158,18 @@
         acts,
         w_section,
     )
-    kind = jnp.where(section == 0, 0, 1 + section % 2)
     even = lax.switch(
-        kind,
+        jnp.where(section == 0, 0, 1 + section % 2),
         (
             lambda: (front[0], *updated(front[1], *parts, slots)),
             lambda: chain(near, slope, acts_t),
             nothing,
         ),
     )
-    out = lax.cond(section % 2 == 0, lambda: even, lambda: chain(far, slope, acts_t))
+    out = lax.switch(
+        jnp.where(section == sections - 1, 2, section % 2),
+        (lambda: even, lambda: chain(far, slope, acts_t), lambda: chain(around, slope, acts_t)),
+    )
     return tuple(x[None] for x in out)
 
 

time: 74.9 us -> 80.5 us (1.075)
  starting transfers between devices: 27.4 us -> 30.2 us
  other arithmetic: 0.27 us -> 2.07 us
  local copies, waits for them, and re-layouts: 3.57 us -> 4.86 us
    cond x6 -> x8, local copies, waits for them, and re-layouts: 1.7 us -> 4.02 us
    sub x1, other arithmetic: 0.27 us -> 2.07 us  [updated(): master_out = master_section - 0.01 * (direction + 0.1 * master_section)]
    ppermute x1 -> x2, starting transfers between devices: 22.1 us -> 23.5 us  [the longest x1 22.1 us: local(): around = lax.ppermute(block, 'pipe', [(0, sections - 1)])]
    unnamed x18 -> x6, local copies, waits for them, and re-layouts: 1.83 us -> 0.8 us
  transfers between devices with their start and end apart: 4 -> 5, of which waited for: 1 -> 1; matrix products, arithmetic and copies ran while one was open for 43% -> 44% of each run, Pallas kernels for 8% -> 8%
where the time goes in v5:
time: 80.5 us; the launch traced here: 80.1 us
  blocking collectives  34.8 us (43%)
  starting transfers between devices  30.2 us (38%)
  Pallas kernels  6.56 us (8%)
  local copies, waits for them, and re-layouts  4.86 us (6%)
  other arithmetic  2.07 us (3%)
    cond x1, blocking collectives  29.2 us
    ppermute x1, starting transfers between devices, local(): around = lax.ppermute(block, 'pipe', [(0, sections - 1)])  22.1 us
    all_gather x1, blocking collectives, updated(): lax.all_gather(other, 'x_lo')  5.64 us
    cond x8, local copies, waits for them, and re-layouts  4.02 us
    cond x1, starting transfers between devices  3.95 us
    pallas_call x1, Pallas kernels, prepared(): pl.pallas_call(prepare, out_shape=(jax.ShapeDtypeStruct((rows, width), jn...  3.21 us
    sub x1, other arithmetic, updated(): master_out = master_section - 0.01 * (direction + 0.1 * master_section)  2.07 us
    pallas_call x1, Pallas kernels, weight_gradient(): pl.pallas_call(weight_term, out_shape=(jax.ShapeDtypeStruct((rows, width)...  1.82 us
  transfers between devices with their start and end apart: 5, of which 1 were waited for; matrix products, arithmetic and copies ran while one was open for 44% of the time, Pallas kernels for 8%

profile of v5, /device:TPU:16, one launch (start us, length us, event | category | flops | bytes accessed | tf_op | source)
XLA Modules:
  0.0 80.1 jit_solution(15886377375114557075)
XLA Ops:
  0.6 1.3 %collective-permute-start.4 = (bf16[256,1024]{1,0:T(8,128)(2,1)}, bf16[256,1024]{1,0:T(8,128)(2,1)S(1)}, u32[]{:S(2)}, u32[]{:S(2)}) collective-permute-start(bf16[256,1024]{1,0:T(8,128)(2,1)} %bitcast.102), channel_id=1, source_target_pairs={{16,0},{17,1},{18,2},{19,3},{20,4},{21,5},{22,6},{23,7},{24,8},{25... | collective-permute-start | bytes 1572872 | tf_op jit(solution)/shard_map/ppermute | solution.py:144
  1.9 1.5 %collective-permute-start.5 = (bf16[256,1024]{1,0:T(8,128)(2,1)}, bf16[256,1024]{1,0:T(8,128)(2,1)}, u32[]{:S(2)}, u32[]{:S(2)}) collective-permute-start(bf16[256,1024]{1,0:T(8,128)(2,1)} %bitcast.103), channel_id=1, source_target_pairs={{48,32},{80,64},{112,96},{144,128},{176,160},{208,192},{240,224},{... | collective-permute-start | bytes 1572872 | tf_op jit(solution)/shard_map/ppermute | solution.py:152
  3.4 1.4 %collective-permute-start.6 = (bf16[256,1024]{1,0:T(8,128)(2,1)}, bf16[256,1024]{1,0:T(8,128)(2,1)}, u32[]{:S(2)}, u32[]{:S(2)}) collective-permute-start(bf16[256,1024]{1,0:T(8,128)(2,1)} %bitcast.104), channel_id=1, source_target_pairs={{32,16},{64,48},{96,80},{128,112},{160,144},{192,176},{224,208},{2... | collective-permute-start | bytes 1572872 | tf_op jit(solution)/shard_map/ppermute | solution.py:143
  4.8 22.1 %collective-permute-start.7 = (bf16[256,1024]{1,0:T(8,128)(2,1)}, bf16[256,1024]{1,0:T(8,128)(2,1)}, u32[]{:S(2)}, u32[]{:S(2)}) collective-permute-start(bf16[256,1024]{1,0:T(8,128)(2,1)} %bitcast.105), channel_id=1, source_target_pairs={{0,1008},{1,1009},{2,1010},{3,1011},{4,1012},{5,1013},{6,1014},{7,... | collective-permute-start | bytes 1572872 | tf_op jit(solution)/shard_map/ppermute | solution.py:151
  26.9 0.0 copy-start.3
  26.9 0.0 copy-start.1
  26.9 0.0 collective-permute-done.4
  26.9 0.0 copy-start.4
  26.9 0.8 copy-done.3
  27.7 6.6 %conditional.4 = (bf16[256,1024]{1,0:T(8,128)(2,1)}, bf16[1080,1024]{1,0:T(8,128)(2,1)S(1)}) conditional(s32[]{:T(128)} %convert_element_type.40, () %tuple.57, (s32[2]{0:T(128)}, bf16[256,1024]{1,0:T(8,128)(2,1)}, bf16[1024,1024]{1,0:T(8,128)(2,1)}, bf16[256,1024]{1,0:T(8,128)(2,1)S(1)}) %tuple.126), branch_computations={%region_0.0_spmd, %region_1.0_spmd} | conditional | flops 536870912 | bytes 13631560 | solution.py:145
  27.7 0.0 copy-start.15
  27.7 0.0 copy-start
  27.7 3.2 %prepare.2 = (f32[256,1024]{1,0:T(8,128)S(1)}, bf16[1080,256]{1,0:T(8,128)(2,1)S(1)}) custom-call(s32[2]{0:T(128)} %get-tuple-element.83.counts_ref, bf16[256,1024]{1,0:T(8,128)(2,1)} %get-tuple-element.84.acts_ref, bf16[1024,1024]{1,0:T(8,128)(2,1)} %get-tuple-element.85.w_ref), custom_call_target="tpu_custom_call" | custom-call | tf_op jit(solution)/shard_map/cond/branch_1_fun/prepare/pallas_call | solution.py:65
  30.9 0.0 copy-done.15
  30.9 1.8 %weight_term.4 = (bf16[256,1024]{1,0:T(8,128)(2,1)S(1)}, bf16[1080,1024]{1,0:T(8,128)(2,1)S(1)}) custom-call(bf16[256,1024]{1,0:T(8,128)(2,1)} %copy-done.15, f32[256,1024]{1,0:T(8,128)S(1)} %get-tuple-element.86.slope_ref, bf16[1080,256]{1,0:T(8,128)(2,1)S(1)} %get-tuple-element.87.acts_t_ref), custom_call_target="tpu_custom_call" | custom-call | tf_op jit(solution)/shard_map/cond/branch_1_fun/weight_term/pallas_call | solution.py:80
  32.8 0.0 copy-done
  32.8 1.5 %input_term.4 = bf16[256,1024]{1,0:T(8,128)(2,1)} custom-call(bf16[256,1024]{1,0:T(8,128)(2,1)S(1)} %get-tuple-element.88.lg_ref, bf16[1024,1024]{1,0:T(8,128)(2,1)S(1)} %copy-done), custom_call_target="tpu_custom_call" | custom-call | flops 536870912 | bytes 3145728 | tf_op jit(solution)/shard_map/cond/branch_1_fun/input_term/pallas_call | solution.py:95
  34.3 0.0 collective-permute-done.5
  34.3 0.0 copy-done.4
  34.3 0.0 copy-done.1
  34.3 45.8 %conditional.6 = (bf16[256,1024]{1,0:T(8,128)(2,1)}, f32[64,1024]{1,0:T(8,128)}, f32[64,1024]{1,0:T(8,128)}, f32[64,1024]{1,0:T(8,128)}) conditional(s32[]{:T(128)} %clamp.7, (f32[64,1024]{1,0:T(8,128)S(1)}, bf16[1080,1024]{1,0:T(8,128)(2,1)S(1)}, f32[64,1024]{1,0:T(8,128)}, f32[64,1024]{1,0:T(8,128)}, ...), branch_computations={%region_4.6_spmd, %region_6.8_spmd, %region_8.9_spmd} | conditional | flops 539230208 | bytes 17875422 | solution.py:161
  34.3 29.2 %fusion = bf16[136,1024]{1,0:T(8,128)(2,1)} fusion(bf16[1080,1024]{1,0:T(8,128)(2,1)S(1)} %get-tuple-element.96), kind=kCustom, calls=%all-reduce-scatter | all-reduce-scatter fusion | flops 1114113 | bytes 2494464 | tf_op jit(solution)/shard_map/cond
  63.5 0.7 slice
  64.2 4.0 %collective-permute-start.2 = (bf16[7,1024]{1,0:T(8,128)(2,1)S(1)}, bf16[7,1024]{1,0:T(8,128)(2,1)S(1)}, u32[]{:S(2)}, u32[]{:S(2)}) collective-permute-start(bf16[7,1024]{1,0:T(8,128)(2,1)S(1)} %slice), channel_id=1, source_target_pairs={{0,1},{1,2},{2,3},{3,4},{4,5},{5,6},{6,7},{8,9},{9,10},{10,11},{11... | collective-permute-start | bytes 43016 | tf_op jit(solution)/shard_map/cond
  68.2 1.3 %dynamic-slice.10 = u32[1]{0:T(128)} dynamic-slice(u32[1024]{0:T(1024)} %constant.212, u32[]{:S(6)} %partition-id.17), dynamic_slice_sizes={1} | dynamic-slice | bytes 12 | tf_op jit(solution)/shard_map/cond
  70.1 0.2 collective-permute-done.2
  70.3 1.9 %concatenate = bf16[143,1024]{1,0:T(8,128)(2,1)S(1)} concatenate(bf16[7,1024]{1,0:T(8,128)(2,1)S(1)} %collective-permute-done.2, bf16[136,1024]{1,0:T(8,128)(2,1)} %fusion), dimensions={0} | concatenate | bytes 585728 | tf_op jit(solution)/shard_map/cond
  72.3 0.1 constant_dynamic-slice_fusion
  72.4 5.6 %all-gather = bf16[128,1024]{1,0:T(8,128)(2,1)S(1)} all-gather(bf16[64,1024]{1,0:T(8,128)(2,1)S(1)} %constant_dynamic-slice_fusion.1), channel_id=2, replica_groups=mesh['pipe'=64,'x_lo'=2,'y'=8] {'x_lo'}, dimensions={0}, use_global_device_ids=true | all-gather | bytes 393216 | tf_op jit(solution)/shard_map/cond/branch_0_fun/all_gather | solution.py:112
  78.0 2.1 %multiply_subtract_fusion = (f32[64,1024]{1,0:T(8,128)}, f32[64,1024]{1,0:T(8,128)}, f32[64,1024]{1,0:T(8,128)}) fusion(f32[64,1024]{1,0:T(8,128)} %get-tuple-element.94, bf16[2,64,1024]{2,1,0:T(8,128)(2,1)S(1)} %bitcast.97, s32[]{:T(128)S(6)} %select_n.40, bf16[135,1024]{1,0:T(8,128)(2,1)S(1)} %constant_dynamic-slice_fusion, s32[]{:T(128)S(6)} %select_n.38, ...), kind=kLoop, calls=%fused_computation.1 | loop fusion | flops 1245184 | bytes 1835016 | tf_op jit(solution)/shard_map/cond/branch_0_fun/sub | solution.py:118
  80.1 0.0 collective-permute-done.6
  80.1 0.0 collective-permute-done.7
  (5 shorter events, 0.1 us)
Async XLA Ops:
  0.6 26.3 %collective-permute-start.4 = (bf16[256,1024]{1,0:T(8,128)(2,1)}, bf16[256,1024]{1,0:T(8,128)(2,1)S(1)}, u32[]{:S(2)}, u32[]{:S(2)}) collective-permute-start(bf16[256,1024]{1,0:T(8,128)(2,1)} %bitcast.102), channel_id=1, source_target_pairs={{16,0},{17,1},{18,2},{19,3},{20,4},{21,5},{22,6},{23,7},{24,8},{25... | collective-permute-start | bytes 1572872 | tf_op jit(solution)/shard_map/ppermute | solution.py:144
  1.9 32.4 %collective-permute-start.5 = (bf16[256,1024]{1,0:T(8,128)(2,1)}, bf16[256,1024]{1,0:T(8,128)(2,1)}, u32[]{:S(2)}, u32[]{:S(2)}) collective-permute-start(bf16[256,1024]{1,0:T(8,128)(2,1)} %bitcast.103), channel_id=1, source_target_pairs={{48,32},{80,64},{112,96},{144,128},{176,160},{208,192},{240,224},{... | collective-permute-start | bytes 1572872 | tf_op jit(solution)/shard_map/ppermute | solution.py:152
  3.4 76.7 %collective-permute-start.6 = (bf16[256,1024]{1,0:T(8,128)(2,1)}, bf16[256,1024]{1,0:T(8,128)(2,1)}, u32[]{:S(2)}, u32[]{:S(2)}) collective-permute-start(bf16[256,1024]{1,0:T(8,128)(2,1)} %bitcast.104), channel_id=1, source_target_pairs={{32,16},{64,48},{96,80},{128,112},{160,144},{192,176},{224,208},{2... | collective-permute-start | bytes 1572872 | tf_op jit(solution)/shard_map/ppermute | solution.py:143
  4.8 75.3 %collective-permute-start.7 = (bf16[256,1024]{1,0:T(8,128)(2,1)}, bf16[256,1024]{1,0:T(8,128)(2,1)}, u32[]{:S(2)}, u32[]{:S(2)}) collective-permute-start(bf16[256,1024]{1,0:T(8,128)(2,1)} %bitcast.105), channel_id=1, source_target_pairs={{0,1008},{1,1009},{2,1010},{3,1011},{4,1012},{5,1013},{6,1014},{7,... | collective-permute-start | bytes 1572872 | tf_op jit(solution)/shard_map/ppermute | solution.py:151
  26.9 0.8 %copy-start.3 = (bf16[1080,256]{1,0:T(8,128)(2,1)}, bf16[1080,256]{1,0:T(8,128)(2,1)S(1)}, u32[]{:S(2)}) copy-start(bf16[1080,256]{1,0:T(8,128)(2,1)S(1)} %get-tuple-element.140) | copy-start | bytes 1658884
  26.9 7.4 %copy-start.1 = (f32[256,1024]{1,0:T(8,128)}, f32[256,1024]{1,0:T(8,128)S(1)}, u32[]{:S(2)}) copy-start(f32[256,1024]{1,0:T(8,128)S(1)} %get-tuple-element.139) | copy-start | bytes 3145732
  26.9 7.4 %copy-start.4 = (f32[1,64,1024]{2,1,0:T(8,128)S(1)}, f32[1,64,1024]{2,1,0:T(8,128)}, u32[]{:S(2)}) copy-start(f32[1,64,1024]{2,1,0:T(8,128)} %param.21) | copy-start | bytes 786436
  27.7 3.2 %copy-start.15 = (bf16[256,1024]{1,0:T(8,128)(2,1)}, bf16[256,1024]{1,0:T(8,128)(2,1)S(1)}, u32[]{:S(2)}) copy-start(bf16[256,1024]{1,0:T(8,128)(2,1)S(1)} %get-tuple-element.82.up_ref) | copy-start | bytes 1572868 | tf_op jit(solution)/shard_map/cond
  27.7 5.1 %copy-start = (bf16[1024,1024]{1,0:T(8,128)(2,1)S(1)}, bf16[1024,1024]{1,0:T(8,128)(2,1)}, u32[]{:S(2)}) copy-start(bf16[1024,1024]{1,0:T(8,128)(2,1)} %get-tuple-element.85.w_ref) | copy-start | bytes 6291460 | tf_op jit(solution)/shard_map/cond
  64.2 6.1 %collective-permute-start.2 = (bf16[7,1024]{1,0:T(8,128)(2,1)S(1)}, bf16[7,1024]{1,0:T(8,128)(2,1)S(1)}, u32[]{:S(2)}, u32[]{:S(2)}) collective-permute-start(bf16[7,1024]{1,0:T(8,128)(2,1)S(1)} %slice), channel_id=1, source_target_pairs={{0,1},{1,2},{2,3},{3,4},{4,5},{5,6},{6,7},{8,9},{9,10},{10,11},{11... | collective-permute-start | bytes 43016 | tf_op jit(solution)/shard_map/cond

commit v6 on v5

--- a/solution.py
+++ b/solution.py
@@ -14,6 +14,7 @@
 X_LO = 2
 COLUMNS = 8
 SPACER = 8
+HALVES = 2
 VMEM = pl.BlockSpec(memory_space=pltpu.VMEM)
 
 
@@ -38,16 +39,24 @@
         slope_ref[at, :] = jnp.where(live, back(jnp.ones_like(pre))[0], jnp.float32(0.0))
 
 
-def weight_term(up_ref, slope_ref, acts_t_ref, lg_ref, total_ref):
+def local_terms(up_ref, slope_ref, acts_t_ref, w_ref, total_ref, in_grad_ref, held_w, held_out, sems):
+    load = pltpu.make_async_copy(w_ref, held_w, sems.at[HALVES])
+    load.start()
     lg = (up_ref[...].astype(jnp.float32) * slope_ref[...]).astype(jnp.bfloat16)
-    lg_ref[...] = lg
     total_ref[...] = jnp.dot(acts_t_ref[...], lg, preferred_element_type=jnp.float32).astype(jnp.bfloat16)
-
-
-def input_term(lg_ref, w_ref, in_grad_ref):
-    in_grad_ref[...] = lax.dot_general(
-        lg_ref[...], w_ref[...], (((1,), (1,)), ((), ())), preferred_element_type=jnp.float32
-    ).astype(jnp.bfloat16)
+    load.wait()
+    half = lg.shape[0] // HALVES
+    stores = []
+    for i in range(HALVES):
+        at = slice(i * half, (i + 1) * half)
+        held_out[at, :] = lax.dot_general(
+            lg[at, :], held_w[...], (((1,), (1,)), ((), ())), preferred_element_type=jnp.float32
+        ).astype(jnp.bfloat16)
+        rows = pl.ds(i * half, half)
+        stores.append(pltpu.make_async_copy(held_out.at[rows, :], in_grad_ref.at[rows, :], sems.at[i]))
+        stores[-1].start()
+    for store in stores:
+        store.wait()
 
 
 def unwritten(ref):
@@ -75,32 +84,26 @@
     )(counts, acts, w_section)
 
 
-def weight_gradient(upstream, slope, acts_t):
+def local_gradients(upstream, slope, acts_t, w_section):
     rows, width = upstream.shape
-    return pl.pallas_call(
-        weight_term,
+    anywhere = pl.BlockSpec(memory_space=pl.ANY)
+    total, in_grad = pl.pallas_call(
+        local_terms,
         out_shape=(
+            jax.ShapeDtypeStruct((acts_t.shape[0], width), jnp.bfloat16),
             jax.ShapeDtypeStruct((rows, width), jnp.bfloat16),
-            jax.ShapeDtypeStruct((acts_t.shape[0], width), jnp.bfloat16),
         ),
-        in_specs=[VMEM] * 3,
-        out_specs=(VMEM, VMEM),
+        in_specs=[VMEM, VMEM, VMEM, anywhere],
+        out_specs=(VMEM, anywhere),
+        scratch_shapes=[
+            pltpu.VMEM(w_section.shape, jnp.bfloat16),
+            pltpu.VMEM((rows, width), jnp.bfloat16),
+            pltpu.SemaphoreType.DMA((HALVES + 1,)),
+        ],
         compiler_params=pltpu.CompilerParams(vmem_limit_bytes=24 * 1024 * 1024),
-        name="weight_term",
-    )(upstream, slope, acts_t)
-
-
-def input_gradient(local_grad, w_section):
-    rows, width = local_grad.shape
-    return pl.pallas_call(
-        input_term,
-        out_shape=jax.ShapeDtypeStruct((rows, width), jnp.bfloat16),
-        in_specs=[VMEM] * 2,
-        out_specs=VMEM,
-        cost_estimate=pl.CostEstimate(flops=2 * rows * width * width, bytes_accessed=3 << 20, transcendentals=0),
-        compiler_params=pltpu.CompilerParams(vmem_limit_bytes=24 * 1024 * 1024),
-        name="input_term",
-    )(local_grad, w_section)
+        name="local_terms",
+    )(upstream, slope, acts_t, w_section)
+    return in_grad, total
 
 
 def updated(total, master_section, first, second, slots):
@@ -129,35 +132,31 @@
     padded = width + (COLUMNS - 1) * SPACER
 
     def chain(upstream, slope, acts_t):
-        local_grad, total = weight_gradient(upstream, slope, acts_t)
-        new = updated(total, *parts, slots)
-        return (input_gradient(local_grad, w_section), *new)
-
-    def first_front(upstream):
-        local_grad, total = weight_gradient(upstream, *prepared(counts, acts, w_section))
-        return input_gradient(local_grad, w_section), total
+        in_grad, total = local_gradients(upstream, slope, acts_t, w_section)
+        return (in_grad, *updated(total, *parts, slots))
 
     def nothing():
         return (blank((rows, width), jnp.bfloat16), *(blank(p.shape, p.dtype) for p in parts))
 
     far = lax.ppermute(block, "pipe", [(s, s - 1) for s in range(2, sections, 2)])
+    inputs = (counts, acts, w_section)
+    ready = lax.cond(
+        section == 1,
+        prepared,
+        lambda *_: (blank((rows, width), jnp.float32), blank((padded, rows), jnp.bfloat16)),
+        *inputs,
+    )
     own = lax.ppermute(block, "pipe", [(1, 0)])
+    ready = lax.cond(section == 0, prepared, lambda *_: ready, *inputs)
     front = lax.cond(
         section == 0,
-        first_front,
+        lambda upstream: local_gradients(upstream, *ready, w_section),
         lambda _: (blank((rows, width), jnp.bfloat16), blank((padded, width), jnp.bfloat16)),
         own,
     )
     around = lax.ppermute(block, "pipe", [(0, sections - 1)])
     near = lax.ppermute(block, "pipe", [(s, s - 1) for s in range(3, sections, 2)])
-    slope, acts_t = lax.cond(
-        section == 0,
-        lambda *_: (blank((rows, width), jnp.float32), blank((padded, rows), jnp.bfloat16)),
-        prepared,
-        counts,
-        acts,
-        w_section,
-    )
+    slope, acts_t = lax.cond(section <= 1, lambda *_: ready, prepared, *inputs)
     even = lax.switch(
         jnp.where(section == 0, 0, 1 + section % 2),
         (

time: 80.5 us -> 80.9 us (level)
  Pallas kernels: 6.56 us -> 10.1 us
  local copies, waits for them, and re-layouts: 4.86 us -> 1.9 us
  other arithmetic: 2.07 us -> 1.05 us
    pallas_call x2 -> x1, Pallas kernels: 3.35 us -> 7.1 us  [local_gradients(): pl.pallas_call(local_terms, out_shape=(jax.ShapeDtypeStruct((acts_t.shape...]
    cond x8 -> x10, local copies, waits for them, and re-layouts: 4.02 us -> 1.85 us
    sub x1, other arithmetic: 2.07 us -> 1.05 us  [updated(): master_out = master_section - 0.01 * (direction + 0.1 * master_section)]
  transfers between devices with their start and end apart: 5 -> 5, of which waited for: 1 -> 1; matrix products, arithmetic and copies ran while one was open for 44% -> 40% of each run, Pallas kernels for 8% -> 13%
where the time goes in v6:
time: 80.9 us; the launch traced here: 80.5 us
  blocking collectives  34.8 us (43%)
  starting transfers between devices  30.2 us (37%)
  Pallas kernels  10.1 us (12%)
  local copies, waits for them, and re-layouts  1.9 us (2%)
  other arithmetic  1.05 us (1%)
  loops' own time  1.01 us (1%)
  between operations  0.89 us (1%)
    cond x1, blocking collectives  29.2 us
    ppermute x1, starting transfers between devices, local(): around = lax.ppermute(block, 'pipe', [(0, sections - 1)])  22.8 us
    pallas_call x1, Pallas kernels, local_gradients(): pl.pallas_call(local_terms, out_shape=(jax.ShapeDtypeStruct((acts_t.shape...  7.1 us
    all_gather x1, blocking collectives, updated(): lax.all_gather(other, 'x_lo')  5.64 us
    cond x1, starting transfers between devices  3.21 us
    pallas_call x1, Pallas kernels, prepared(): pl.pallas_call(prepare, out_shape=(jax.ShapeDtypeStruct((rows, width), jn...  2.98 us
    cond x10, local copies, waits for them, and re-layouts  1.85 us
  transfers between devices with their start and end apart: 5, of which 1 were waited for; matrix products, arithmetic and copies ran while one was open for 40% of the time, Pallas kernels for 13%

profile of v6, /device:TPU:16, one launch (start us, length us, event | category | flops | bytes accessed | tf_op | source)
XLA Modules:
  0.0 80.5 jit_solution(13641465826399038054)
XLA Ops:
  0.6 1.3 %collective-permute-start.4 = (bf16[256,1024]{1,0:T(8,128)(2,1)}, bf16[256,1024]{1,0:T(8,128)(2,1)}, u32[]{:S(2)}, u32[]{:S(2)}) collective-permute-start(bf16[256,1024]{1,0:T(8,128)(2,1)} %bitcast.102), channel_id=1, source_target_pairs={{16,0},{17,1},{18,2},{19,3},{20,4},{21,5},{22,6},{23,7},{24,8},{25... | collective-permute-start | bytes 1572872 | tf_op jit(solution)/shard_map/ppermute | solution.py:149
  1.9 1.5 %collective-permute-start.5 = (bf16[256,1024]{1,0:T(8,128)(2,1)}, bf16[256,1024]{1,0:T(8,128)(2,1)}, u32[]{:S(2)}, u32[]{:S(2)}) collective-permute-start(bf16[256,1024]{1,0:T(8,128)(2,1)} %bitcast.103), channel_id=1, source_target_pairs={{48,32},{80,64},{112,96},{144,128},{176,160},{208,192},{240,224},{... | collective-permute-start | bytes 1572872 | tf_op jit(solution)/shard_map/ppermute | solution.py:158
  3.4 1.4 %collective-permute-start.6 = (bf16[256,1024]{1,0:T(8,128)(2,1)}, bf16[256,1024]{1,0:T(8,128)(2,1)}, u32[]{:S(2)}, u32[]{:S(2)}) collective-permute-start(bf16[256,1024]{1,0:T(8,128)(2,1)} %bitcast.104), channel_id=1, source_target_pairs={{32,16},{64,48},{96,80},{128,112},{160,144},{192,176},{224,208},{2... | collective-permute-start | bytes 1572872 | tf_op jit(solution)/shard_map/ppermute | solution.py:141
  4.8 22.8 %collective-permute-start.7 = (bf16[256,1024]{1,0:T(8,128)(2,1)}, bf16[256,1024]{1,0:T(8,128)(2,1)}, u32[]{:S(2)}, u32[]{:S(2)}) collective-permute-start(bf16[256,1024]{1,0:T(8,128)(2,1)} %bitcast.105), channel_id=1, source_target_pairs={{0,1008},{1,1009},{2,1010},{3,1011},{4,1012},{5,1013},{6,1014},{7,... | collective-permute-start | bytes 1572872 | tf_op jit(solution)/shard_map/ppermute | solution.py:157
  27.6 3.0 %conditional.7 = ((f32[256,1024]{1,0:T(8,128)S(1)}, bf16[1080,256]{1,0:T(8,128)(2,1)S(1)})) conditional(s32[]{:T(128)} %convert_element_type.46, (f32[256,1024]{1,0:T(8,128)S(1)}, bf16[1080,256]{1,0:T(8,128)(2,1)S(1)}) %get-tuple-element.237, (s32[2]{0:T(128)}, bf16[256,1024]{1,0:T(8,128)(2,1)}, bf16[1024,1024]{1,0:T(8,128)(2,1)}) %tuple.131), branch_computations={%region_2.0_spmd, %region_3.0_spmd} | conditional | bytes 8 | solution.py:150
  27.6 3.0 %prepare.4 = (f32[256,1024]{1,0:T(8,128)S(1)}, bf16[1080,256]{1,0:T(8,128)(2,1)S(1)}) custom-call(s32[2]{0:T(128)} %get-tuple-element.105.counts_ref, bf16[256,1024]{1,0:T(8,128)(2,1)} %get-tuple-element.106.acts_ref, bf16[1024,1024]{1,0:T(8,128)(2,1)} %get-tuple-element.107.w_ref), custom_call_target="tpu_custom_call" | custom-call | tf_op jit(solution)/shard_map/cond/branch_1_fun/prepare/pallas_call | solution.py:74
  30.6 0.2 conditional.9
  30.6 0.1 copy.25
  30.8 0.0 copy-start
  30.8 0.0 collective-permute-done.4
  30.8 0.0 copy-start.2
  30.8 7.1 %conditional.8 = (bf16[256,1024]{1,0:T(8,128)(2,1)}, bf16[1080,1024]{1,0:T(8,128)(2,1)}) conditional(s32[]{:T(128)} %convert_element_type.46, () %tuple.67, (bf16[256,1024]{1,0:T(8,128)(2,1)}, f32[256,1024]{1,0:T(8,128)S(1)}, bf16[1080,256]{1,0:T(8,128)(2,1)S(1)}, bf16[1024,1024]{1,0:T(8,128)(2,1)}) %tuple.124), branch_computations={%region_4.0_spmd, %region_5.0_spmd} | conditional | bytes 16 | solution.py:151
  30.9 7.1 %local_terms.4 = (bf16[1080,1024]{1,0:T(8,128)(2,1)}, bf16[256,1024]{1,0:T(8,128)(2,1)}) custom-call(bf16[256,1024]{1,0:T(8,128)(2,1)} %get-tuple-element.108.up_ref, f32[256,1024]{1,0:T(8,128)S(1)} %get-tuple-element.109.slope_ref, bf16[1080,256]{1,0:T(8,128)(2,1)S(1)} %get-tuple-element.110.acts_t_ref, bf16[1024,1024]{1,0:T(8,128)(2,1)} %get-tuple-element.111.w_ref), custom_call_target="tpu_custom_call" | custom-call | tf_op jit(solution)/shard_map/cond/branch_1_fun/local_terms/pallas_call | solution.py:90
  38.0 0.0 collective-permute-done.5
  38.0 0.0 copy-done.2
  38.0 0.0 copy-done
  38.0 42.1 %conditional.10 = (bf16[256,1024]{1,0:T(8,128)(2,1)}, f32[64,1024]{1,0:T(8,128)}, f32[64,1024]{1,0:T(8,128)}, f32[64,1024]{1,0:T(8,128)}) conditional(s32[]{:T(128)} %clamp.7, (f32[64,1024]{1,0:T(8,128)S(1)}, bf16[1080,1024]{1,0:T(8,128)(2,1)}, f32[64,1024]{1,0:T(8,128)}, f32[64,1024]{1,0:T(8,128)}, ...), branch_computations={%region_8.10_spmd, %region_10.12_spmd, %region_12.13_spmd} | conditional | flops 2359318 | bytes 8421742 | solution.py:160
  38.0 0.0 copy-start.3
  38.0 0.0 copy-start.6
  38.0 29.2 %fusion = bf16[136,1024]{1,0:T(8,128)(2,1)S(1)} fusion(bf16[1080,1024]{1,0:T(8,128)(2,1)} %get-tuple-element.120), kind=kCustom, calls=%all-reduce-scatter | all-reduce-scatter fusion | flops 1114113 | bytes 2494464 | tf_op jit(solution)/shard_map/cond
  67.3 3.2 %collective-permute-start.2 = (bf16[7,1024]{1,0:T(8,128)(2,1)S(1)}, bf16[7,1024]{1,0:T(8,128)(2,1)S(1)}, u32[]{:S(2)}, u32[]{:S(2)}) collective-permute-start(bf16[7,1024]{1,0:T(8,128)(2,1)S(1)} %slice), channel_id=1, source_target_pairs={{0,1},{1,2},{2,3},{3,4},{4,5},{5,6},{6,7},{8,9},{9,10},{10,11},{11... | collective-permute-start | bytes 43016 | tf_op jit(solution)/shard_map/cond
  70.5 1.3 %dynamic-slice.10 = u32[1]{0:T(128)} dynamic-slice(u32[1024]{0:T(1024)} %constant.212, u32[]{:S(6)} %partition-id.21), dynamic_slice_sizes={1} | dynamic-slice | bytes 12 | tf_op jit(solution)/shard_map/cond
  72.4 0.5 collective-permute-done.2
  72.9 0.3 concatenate
  73.2 0.1 constant_dynamic-slice_fusion
  73.4 5.6 %all-gather = bf16[128,1024]{1,0:T(8,128)(2,1)S(1)} all-gather(bf16[64,1024]{1,0:T(8,128)(2,1)S(1)} %constant_dynamic-slice_fusion.1), channel_id=2, replica_groups=mesh['pipe'=64,'x_lo'=2,'y'=8] {'x_lo'}, dimensions={0}, use_global_device_ids=true | all-gather | bytes 393216 | tf_op jit(solution)/shard_map/cond/branch_0_fun/all_gather | solution.py:115
  79.0 0.0 copy-done.3
  79.0 0.0 copy-done.6
  79.0 1.0 %multiply_subtract_fusion = (f32[64,1024]{1,0:T(8,128)}, f32[64,1024]{1,0:T(8,128)}, f32[64,1024]{1,0:T(8,128)}) fusion(f32[64,1024]{1,0:T(8,128)S(1)} %copy-done.6, bf16[2,64,1024]{2,1,0:T(8,128)(2,1)S(1)} %bitcast.100, s32[]{:T(128)S(6)} %select_n.40, bf16[135,1024]{1,0:T(8,128)(2,1)S(1)} %constant_dynamic-slice_fusion, s32[]{:T(128)S(6)} %select_n.38, ...), kind=kLoop, calls=%fused_computation.1 | loop fusion | flops 1245184 | bytes 1835016 | tf_op jit(solution)/shard_map/cond/branch_0_fun/sub | solution.py:121
  80.1 0.0 collective-permute-done.6
  80.1 0.0 collective-permute-done.7
  80.1 0.2 conditional.11
  (6 shorter events, 0.1 us)
Async XLA Ops:
  0.6 30.2 %collective-permute-start.4 = (bf16[256,1024]{1,0:T(8,128)(2,1)}, bf16[256,1024]{1,0:T(8,128)(2,1)}, u32[]{:S(2)}, u32[]{:S(2)}) collective-permute-start(bf16[256,1024]{1,0:T(8,128)(2,1)} %bitcast.102), channel_id=1, source_target_pairs={{16,0},{17,1},{18,2},{19,3},{20,4},{21,5},{22,6},{23,7},{24,8},{25... | collective-permute-start | bytes 1572872 | tf_op jit(solution)/shard_map/ppermute | solution.py:149
  1.9 36.0 %collective-permute-start.5 = (bf16[256,1024]{1,0:T(8,128)(2,1)}, bf16[256,1024]{1,0:T(8,128)(2,1)}, u32[]{:S(2)}, u32[]{:S(2)}) collective-permute-start(bf16[256,1024]{1,0:T(8,128)(2,1)} %bitcast.103), channel_id=1, source_target_pairs={{48,32},{80,64},{112,96},{144,128},{176,160},{208,192},{240,224},{... | collective-permute-start | bytes 1572872 | tf_op jit(solution)/shard_map/ppermute | solution.py:158
  3.4 76.7 %collective-permute-start.6 = (bf16[256,1024]{1,0:T(8,128)(2,1)}, bf16[256,1024]{1,0:T(8,128)(2,1)}, u32[]{:S(2)}, u32[]{:S(2)}) collective-permute-start(bf16[256,1024]{1,0:T(8,128)(2,1)} %bitcast.104), channel_id=1, source_target_pairs={{32,16},{64,48},{96,80},{128,112},{160,144},{192,176},{224,208},{2... | collective-permute-start | bytes 1572872 | tf_op jit(solution)/shard_map/ppermute | solution.py:141
  4.8 75.2 %collective-permute-start.7 = (bf16[256,1024]{1,0:T(8,128)(2,1)}, bf16[256,1024]{1,0:T(8,128)(2,1)}, u32[]{:S(2)}, u32[]{:S(2)}) collective-permute-start(bf16[256,1024]{1,0:T(8,128)(2,1)} %bitcast.105), channel_id=1, source_target_pairs={{0,1008},{1,1009},{2,1010},{3,1011},{4,1012},{5,1013},{6,1014},{7,... | collective-permute-start | bytes 1572872 | tf_op jit(solution)/shard_map/ppermute | solution.py:157
  30.8 7.2 %copy-start = (bf16[1080,256]{1,0:T(8,128)(2,1)}, bf16[1080,256]{1,0:T(8,128)(2,1)S(1)}, u32[]{:S(2)}) copy-start(bf16[1080,256]{1,0:T(8,128)(2,1)S(1)} %get-tuple-element.168) | copy-start | bytes 1658884
  30.8 7.2 %copy-start.2 = (f32[1,64,1024]{2,1,0:T(8,128)S(1)}, f32[1,64,1024]{2,1,0:T(8,128)}, u32[]{:S(2)}) copy-start(f32[1,64,1024]{2,1,0:T(8,128)} %param.25) | copy-start | bytes 786436
  38.0 41.0 %copy-start.3 = (f32[64,1024]{1,0:T(8,128)S(1)}, f32[64,1024]{1,0:T(8,128)}, u32[]{:S(2)}) copy-start(f32[64,1024]{1,0:T(8,128)} %get-tuple-element.121) | copy-start | bytes 786436 | tf_op jit(solution)/shard_map/cond
  38.0 41.0 %copy-start.6 = (f32[64,1024]{1,0:T(8,128)S(1)}, f32[64,1024]{1,0:T(8,128)}, u32[]{:S(2)}) copy-start(f32[64,1024]{1,0:T(8,128)} %get-tuple-element.118) | copy-start | bytes 786436 | tf_op jit(solution)/shard_map/cond
  67.3 5.6 %collective-permute-start.2 = (bf16[7,1024]{1,0:T(8,128)(2,1)S(1)}, bf16[7,1024]{1,0:T(8,128)(2,1)S(1)}, u32[]{:S(2)}, u32[]{:S(2)}) collective-permute-start(bf16[7,1024]{1,0:T(8,128)(2,1)S(1)} %slice), channel_id=1, source_target_pairs={{0,1},{1,2},{2,3},{3,4},{4,5},{5,6},{6,7},{8,9},{9,10},{10,11},{11... | collective-permute-start | bytes 43016 | tf_op jit(solution)/shard_map/cond

commit v7 on v5

--- a/solution.py
+++ b/solution.py
@@ -133,31 +133,32 @@
         new = updated(total, *parts, slots)
         return (input_gradient(local_grad, w_section), *new)
 
-    def first_front(upstream):
-        local_grad, total = weight_gradient(upstream, *prepared(counts, acts, w_section))
+    def front_of_first(upstream, slope, acts_t):
+        local_grad, total = weight_gradient(upstream, slope, acts_t)
         return input_gradient(local_grad, w_section), total
 
     def nothing():
         return (blank((rows, width), jnp.bfloat16), *(blank(p.shape, p.dtype) for p in parts))
 
     far = lax.ppermute(block, "pipe", [(s, s - 1) for s in range(2, sections, 2)])
+    inputs = (counts, acts, w_section)
+    ready = lax.cond(
+        section == 1,
+        prepared,
+        lambda *_: (blank((rows, width), jnp.float32), blank((padded, rows), jnp.bfloat16)),
+        *inputs,
+    )
     own = lax.ppermute(block, "pipe", [(1, 0)])
+    ready = lax.cond(section == 0, prepared, lambda *_: ready, *inputs)
     front = lax.cond(
         section == 0,
-        first_front,
+        lambda upstream: front_of_first(upstream, *ready),
         lambda _: (blank((rows, width), jnp.bfloat16), blank((padded, width), jnp.bfloat16)),
         own,
     )
     around = lax.ppermute(block, "pipe", [(0, sections - 1)])
     near = lax.ppermute(block, "pipe", [(s, s - 1) for s in range(3, sections, 2)])
-    slope, acts_t = lax.cond(
-        section == 0,
-        lambda *_: (blank((rows, width), jnp.float32), blank((padded, rows), jnp.bfloat16)),
-        prepared,
-        counts,
-        acts,
-        w_section,
-    )
+    slope, acts_t = lax.cond(section <= 1, lambda *_: ready, prepared, *inputs)
     even = lax.switch(
         jnp.where(section == 0, 0, 1 + section % 2),
         (

time: 80.5 us -> 82.6 us (1.026)
  Pallas kernels: 6.56 us -> 7.87 us
  waiting for transfers between devices: 0.19 us -> 1.28 us
  local copies, waits for them, and re-layouts: 4.86 us -> 5.89 us
    cond x1, starting transfers between devices: 3.95 us -> 2.4 us
    pallas_call x1, Pallas kernels: 1.82 us -> 3.35 us  [weight_gradient(): pl.pallas_call(weight_term, out_shape=(jax.ShapeDtypeStruct((rows, width)...]
    cond x1, waiting for transfers between devices: 0.18 us -> 1.27 us
    cond x8 -> x10, local copies, waits for them, and re-layouts: 4.02 us -> 4.24 us
  transfers between devices with their start and end apart: 5 -> 5, of which waited for: 1 -> 1; matrix products, arithmetic and copies ran while one was open for 44% -> 42% of each run, Pallas kernels for 8% -> 10%
where the time goes in v7:
time: 82.6 us; the launch traced here: 82.1 us
  blocking collectives  34.8 us (42%)
  starting transfers between devices  29.5 us (36%)
  Pallas kernels  7.87 us (10%)
  local copies, waits for them, and re-layouts  5.89 us (7%)
  other arithmetic  1.29 us (2%)
  waiting for transfers between devices  1.28 us (2%)
    cond x1, blocking collectives  29.1 us
    ppermute x1, starting transfers between devices, local(): around = lax.ppermute(block, 'pipe', [(0, sections - 1)])  22.8 us
    all_gather x1, blocking collectives, updated(): lax.all_gather(other, 'x_lo')  5.64 us
    cond x10, local copies, waits for them, and re-layouts  4.24 us
    pallas_call x1, Pallas kernels, weight_gradient(): pl.pallas_call(weight_term, out_shape=(jax.ShapeDtypeStruct((rows, width)...  3.35 us
    pallas_call x1, Pallas kernels, prepared(): pl.pallas_call(prepare, out_shape=(jax.ShapeDtypeStruct((rows, width), jn...  2.99 us
    cond x1, starting transfers between devices  2.4 us
  transfers between devices with their start and end apart: 5, of which 1 were waited for; matrix products, arithmetic and copies ran while one was open for 42% of the time, Pallas kernels for 10%

profile of v7, /device:TPU:16, one launch (start us, length us, event | category | flops | bytes accessed | tf_op | source)
XLA Modules:
  0.0 82.1 jit_solution(7509106859851955517)
XLA Ops:
  0.6 1.3 %collective-permute-start.4 = (bf16[256,1024]{1,0:T(8,128)(2,1)}, bf16[256,1024]{1,0:T(8,128)(2,1)}, u32[]{:S(2)}, u32[]{:S(2)}) collective-permute-start(bf16[256,1024]{1,0:T(8,128)(2,1)} %bitcast.108), channel_id=1, source_target_pairs={{16,0},{17,1},{18,2},{19,3},{20,4},{21,5},{22,6},{23,7},{24,8},{25... | collective-permute-start | bytes 1572872 | tf_op jit(solution)/shard_map/ppermute | solution.py:151
  1.9 1.5 %collective-permute-start.5 = (bf16[256,1024]{1,0:T(8,128)(2,1)}, bf16[256,1024]{1,0:T(8,128)(2,1)}, u32[]{:S(2)}, u32[]{:S(2)}) collective-permute-start(bf16[256,1024]{1,0:T(8,128)(2,1)} %bitcast.109), channel_id=1, source_target_pairs={{48,32},{80,64},{112,96},{144,128},{176,160},{208,192},{240,224},{... | collective-permute-start | bytes 1572872 | tf_op jit(solution)/shard_map/ppermute | solution.py:160
  3.4 1.5 %collective-permute-start.6 = (bf16[256,1024]{1,0:T(8,128)(2,1)}, bf16[256,1024]{1,0:T(8,128)(2,1)}, u32[]{:S(2)}, u32[]{:S(2)}) collective-permute-start(bf16[256,1024]{1,0:T(8,128)(2,1)} %bitcast.110), channel_id=1, source_target_pairs={{32,16},{64,48},{96,80},{128,112},{160,144},{192,176},{224,208},{2... | collective-permute-start | bytes 1572872 | tf_op jit(solution)/shard_map/ppermute | solution.py:143
  4.9 22.8 %collective-permute-start.7 = (bf16[256,1024]{1,0:T(8,128)(2,1)}, bf16[256,1024]{1,0:T(8,128)(2,1)}, u32[]{:S(2)}, u32[]{:S(2)}) collective-permute-start(bf16[256,1024]{1,0:T(8,128)(2,1)} %bitcast.111), channel_id=1, source_target_pairs={{0,1008},{1,1009},{2,1010},{3,1011},{4,1012},{5,1013},{6,1014},{7,... | collective-permute-start | bytes 1572872 | tf_op jit(solution)/shard_map/ppermute | solution.py:159
  27.7 3.0 %conditional.7 = ((f32[256,1024]{1,0:T(8,128)S(1)}, bf16[1080,256]{1,0:T(8,128)(2,1)S(1)})) conditional(s32[]{:T(128)} %convert_element_type.46, (f32[256,1024]{1,0:T(8,128)S(1)}, bf16[1080,256]{1,0:T(8,128)(2,1)S(1)}) %get-tuple-element.237, (s32[2]{0:T(128)}, bf16[256,1024]{1,0:T(8,128)(2,1)}, bf16[1024,1024]{1,0:T(8,128)(2,1)}) %tuple.134), branch_computations={%region_2.0_spmd, %region_3.0_spmd} | conditional | bytes 8 | solution.py:152
  27.7 3.0 %prepare.4 = (f32[256,1024]{1,0:T(8,128)S(1)}, bf16[1080,256]{1,0:T(8,128)(2,1)S(1)}) custom-call(s32[2]{0:T(128)} %get-tuple-element.105.counts_ref, bf16[256,1024]{1,0:T(8,128)(2,1)} %get-tuple-element.106.acts_ref, bf16[1024,1024]{1,0:T(8,128)(2,1)} %get-tuple-element.107.w_ref), custom_call_target="tpu_custom_call" | custom-call | tf_op jit(solution)/shard_map/cond/branch_1_fun/prepare/pallas_call | solution.py:65
  30.7 0.2 conditional.9
  30.7 0.1 copy.25
  30.9 0.0 copy-start.4
  30.9 0.0 copy-start.1
  30.9 0.0 collective-permute-done.4
  30.9 0.0 copy-start.5
  30.9 0.8 copy-done.4
  31.7 5.0 %conditional.8 = (bf16[256,1024]{1,0:T(8,128)(2,1)}, bf16[1080,1024]{1,0:T(8,128)(2,1)S(1)}) conditional(s32[]{:T(128)} %convert_element_type.46, () %tuple.67, (bf16[256,1024]{1,0:T(8,128)(2,1)}, f32[256,1024]{1,0:T(8,128)S(1)}, bf16[1080,256]{1,0:T(8,128)(2,1)S(1)}, bf16[1024,1024]{1,0:T(8,128)(2,1)}) %tuple.124), branch_computations={%region_4.0_spmd, %region_5.0_spmd} | conditional | flops 536870912 | bytes 20381768 | solution.py:153
  31.7 0.0 copy-start
  31.7 3.3 %weight_term.4 = (bf16[256,1024]{1,0:T(8,128)(2,1)S(1)}, bf16[1080,1024]{1,0:T(8,128)(2,1)}) custom-call(bf16[256,1024]{1,0:T(8,128)(2,1)} %get-tuple-element.108.up_ref, f32[256,1024]{1,0:T(8,128)S(1)} %get-tuple-element.109.slope_ref, bf16[1080,256]{1,0:T(8,128)(2,1)S(1)} %get-tuple-element.110.acts_t_ref), custom_call_target="tpu_custom_call" | custom-call | tf_op jit(solution)/shard_map/cond/branch_1_fun/weight_term/pallas_call | solution.py:80
  35.0 0.0 copy-start.3
  35.0 0.0 copy-done
  35.0 1.5 %input_term.4 = bf16[256,1024]{1,0:T(8,128)(2,1)} custom-call(bf16[256,1024]{1,0:T(8,128)(2,1)S(1)} %get-tuple-element.111.lg_ref, bf16[1024,1024]{1,0:T(8,128)(2,1)S(1)} %copy-done), custom_call_target="tpu_custom_call" | custom-call | flops 536870912 | bytes 3145728 | tf_op jit(solution)/shard_map/cond/branch_1_fun/input_term/pallas_call | solution.py:95
  36.6 0.1 copy-done.3
  36.7 0.0 collective-permute-done.5
  36.7 0.0 copy-done.5
  36.7 0.0 copy-done.1
  36.7 44.5 %conditional.10 = (bf16[256,1024]{1,0:T(8,128)(2,1)}, f32[64,1024]{1,0:T(8,128)S(1)}, f32[64,1024]{1,0:T(8,128)S(1)}, f32[64,1024]{1,0:T(8,128)S(1)}) conditional(s32[]{:T(128)} %clamp.7, (f32[64,1024]{1,0:T(8,128)S(1)}, bf16[1080,1024]{1,0:T(8,128)(2,1)S(1)}, f32[64,1024]{1,0:T(8,128)}, f32[64,1024]{1,0:T(8,128)}, ...), branch_computations={%region_8.10_spmd, %region_10.12_spmd, %region_12.13_spmd} | conditional | flops 539230208 | bytes 17875422 | solution.py:162
  36.7 29.1 %fusion = bf16[136,1024]{1,0:T(8,128)(2,1)} fusion(bf16[1080,1024]{1,0:T(8,128)(2,1)S(1)} %get-tuple-element.120), kind=kCustom, calls=%all-reduce-scatter | all-reduce-scatter fusion | flops 1114113 | bytes 2494464 | tf_op jit(solution)/shard_map/cond
  65.8 0.7 slice
  66.6 2.4 %collective-permute-start.2 = (bf16[7,1024]{1,0:T(8,128)(2,1)S(1)}, bf16[7,1024]{1,0:T(8,128)(2,1)S(1)}, u32[]{:S(2)}, u32[]{:S(2)}) collective-permute-start(bf16[7,1024]{1,0:T(8,128)(2,1)S(1)} %slice), channel_id=1, source_target_pairs={{0,1},{1,2},{2,3},{3,4},{4,5},{5,6},{6,7},{8,9},{9,10},{10,11},{11... | collective-permute-start | bytes 43016 | tf_op jit(solution)/shard_map/cond
  69.0 1.3 %dynamic-slice.10 = u32[1]{0:T(128)} dynamic-slice(u32[1024]{0:T(1024)} %constant.212, u32[]{:S(6)} %partition-id.21), dynamic_slice_sizes={1} | dynamic-slice | bytes 12 | tf_op jit(solution)/shard_map/cond
  70.9 1.3 %collective-permute-done.2 = bf16[7,1024]{1,0:T(8,128)(2,1)S(1)} collective-permute-done((bf16[7,1024]{1,0:T(8,128)(2,1)S(1)}, bf16[7,1024]{1,0:T(8,128)(2,1)S(1)}, u32[]{:S(2)}, u32[]{:S(2)}) %collective-permute-start.2) | collective-permute-done | bytes 14368 | tf_op jit(solution)/shard_map/cond
  72.2 1.9 %concatenate = bf16[143,1024]{1,0:T(8,128)(2,1)S(1)} concatenate(bf16[7,1024]{1,0:T(8,128)(2,1)S(1)} %collective-permute-done.2, bf16[136,1024]{1,0:T(8,128)(2,1)} %fusion), dimensions={0} | concatenate | bytes 585728 | tf_op jit(solution)/shard_map/cond
  74.1 0.1 constant_dynamic-slice_fusion
  74.3 5.6 %all-gather = bf16[128,1024]{1,0:T(8,128)(2,1)S(1)} all-gather(bf16[64,1024]{1,0:T(8,128)(2,1)S(1)} %constant_dynamic-slice_fusion.1), channel_id=2, replica_groups=mesh['pipe'=64,'x_lo'=2,'y'=8] {'x_lo'}, dimensions={0}, use_global_device_ids=true | all-gather | bytes 393216 | tf_op jit(solution)/shard_map/cond/branch_0_fun/all_gather | solution.py:112
  79.9 1.3 %multiply_subtract_fusion = (f32[64,1024]{1,0:T(8,128)S(1)}, f32[64,1024]{1,0:T(8,128)S(1)}, f32[64,1024]{1,0:T(8,128)S(1)}) fusion(f32[64,1024]{1,0:T(8,128)} %get-tuple-element.118, bf16[2,64,1024]{2,1,0:T(8,128)(2,1)S(1)} %bitcast.100, s32[]{:T(128)S(6)} %select_n.40, bf16[135,1024]{1,0:T(8,128)(2,1)S(1)} %constant_dynamic-slice_fusion, s32[]{:T(128)S(6)} %select_n.38, ...), kind=kLoop, calls=%fused_computation.1 | loop fusion | flops 1245184 | bytes 1835016 | tf_op jit(solution)/shard_map/cond/branch_0_fun/sub | solution.py:118
  81.2 0.0 copy-start.16
  81.2 0.0 copy-start.17
  81.2 0.0 copy-start.18
  81.2 0.0 collective-permute-done.6
  81.2 0.0 collective-permute-done.7
  81.3 0.6 copy-done.16
  81.9 0.1 copy-done.17
  82.0 0.1 copy-done.18
  (6 shorter events, 0.1 us)
Async XLA Ops:
  0.6 30.3 %collective-permute-start.4 = (bf16[256,1024]{1,0:T(8,128)(2,1)}, bf16[256,1024]{1,0:T(8,128)(2,1)}, u32[]{:S(2)}, u32[]{:S(2)}) collective-permute-start(bf16[256,1024]{1,0:T(8,128)(2,1)} %bitcast.108), channel_id=1, source_target_pairs={{16,0},{17,1},{18,2},{19,3},{20,4},{21,5},{22,6},{23,7},{24,8},{25... | collective-permute-start | bytes 1572872 | tf_op jit(solution)/shard_map/ppermute | solution.py:151
  1.9 34.7 %collective-permute-start.5 = (bf16[256,1024]{1,0:T(8,128)(2,1)}, bf16[256,1024]{1,0:T(8,128)(2,1)}, u32[]{:S(2)}, u32[]{:S(2)}) collective-permute-start(bf16[256,1024]{1,0:T(8,128)(2,1)} %bitcast.109), channel_id=1, source_target_pairs={{48,32},{80,64},{112,96},{144,128},{176,160},{208,192},{240,224},{... | collective-permute-start | bytes 1572872 | tf_op jit(solution)/shard_map/ppermute | solution.py:160
  3.4 77.8 %collective-permute-start.6 = (bf16[256,1024]{1,0:T(8,128)(2,1)}, bf16[256,1024]{1,0:T(8,128)(2,1)}, u32[]{:S(2)}, u32[]{:S(2)}) collective-permute-start(bf16[256,1024]{1,0:T(8,128)(2,1)} %bitcast.110), channel_id=1, source_target_pairs={{32,16},{64,48},{96,80},{128,112},{160,144},{192,176},{224,208},{2... | collective-permute-start | bytes 1572872 | tf_op jit(solution)/shard_map/ppermute | solution.py:143
  4.9 76.4 %collective-permute-start.7 = (bf16[256,1024]{1,0:T(8,128)(2,1)}, bf16[256,1024]{1,0:T(8,128)(2,1)}, u32[]{:S(2)}, u32[]{:S(2)}) collective-permute-start(bf16[256,1024]{1,0:T(8,128)(2,1)} %bitcast.111), channel_id=1, source_target_pairs={{0,1008},{1,1009},{2,1010},{3,1011},{4,1012},{5,1013},{6,1014},{7,... | collective-permute-start | bytes 1572872 | tf_op jit(solution)/shard_map/ppermute | solution.py:159
  30.9 0.8 copy-start.4
  30.9 5.8 %copy-start.1 = (f32[256,1024]{1,0:T(8,128)}, f32[256,1024]{1,0:T(8,128)S(1)}, u32[]{:S(2)}) copy-start(f32[256,1024]{1,0:T(8,128)S(1)} %get-tuple-element.167) | copy-start | bytes 3145732
  30.9 5.8 %copy-start.5 = (f32[1,64,1024]{2,1,0:T(8,128)S(1)}, f32[1,64,1024]{2,1,0:T(8,128)}, u32[]{:S(2)}) copy-start(f32[1,64,1024]{2,1,0:T(8,128)} %param.25) | copy-start | bytes 786436
  31.7 3.4 %copy-start = (bf16[1024,1024]{1,0:T(8,128)(2,1)S(1)}, bf16[1024,1024]{1,0:T(8,128)(2,1)}, u32[]{:S(2)}) copy-start(bf16[1024,1024]{1,0:T(8,128)(2,1)} %get-tuple-element.112.w_ref) | copy-start | bytes 6291460 | tf_op jit(solution)/shard_map/cond
  35.0 1.6 %copy-start.3 = (bf16[1080,1024]{1,0:T(8,128)(2,1)S(1)}, bf16[1080,1024]{1,0:T(8,128)(2,1)}, u32[]{:S(2)}) copy-start(bf16[1080,1024]{1,0:T(8,128)(2,1)} %get-tuple-element.204) | copy-start | bytes 6635524 | tf_op jit(solution)/shard_map/cond
  66.6 5.6 %collective-permute-start.2 = (bf16[7,1024]{1,0:T(8,128)(2,1)S(1)}, bf16[7,1024]{1,0:T(8,128)(2,1)S(1)}, u32[]{:S(2)}, u32[]{:S(2)}) collective-permute-start(bf16[7,1024]{1,0:T(8,128)(2,1)S(1)} %slice), channel_id=1, source_target_pairs={{0,1},{1,2},{2,3},{3,4},{4,5},{5,6},{6,7},{8,9},{9,10},{10,11},{11... | collective-permute-start | bytes 43016 | tf_op jit(solution)/shard_map/cond
  81.2 0.7 copy-start.16
  81.2 0.8 copy-start.17
  81.2 0.9 %copy-start.18 = (f32[64,1024]{1,0:T(8,128)}, f32[64,1024]{1,0:T(8,128)S(1)}, u32[]{:S(2)}) copy-start(f32[64,1024]{1,0:T(8,128)S(1)} %get-tuple-element.254) | copy-start | bytes 786436
